TPU v7x, 32 devices: a whole 2x2x4 slice. The times are simulated.
32 devices in a mesh: seq: 8 (over z, x), ch: 4 (over y, core).
Axes of the slice: x: 2, y: 2, z: 4, core: 2. Of those that a mesh axis runs over, the one named last changes fastest.
Arguments:
- x_in: bfloat16 [2048, 2048], P('seq'), may hold values from -6 to 6
- norm_gain: float32 [2048], replicated, may hold values from 0.25 to 1.75
- w_in: bfloat16 [3, 2048, 2, 4096], P(None, None, None, 'ch'), may hold values from -0.125 to 0.125
- conv_weight: float32 [4, 4096], P(None, 'ch'), may hold values from -3 to 3
- conv_bias: float32 [4096], P('ch'), may hold values from -1.5 to 1.5
- x_proj: bfloat16 [4096, 160], P('ch'), may hold values from -0.09375 to 0.09375
- dt_proj: bfloat16 [128, 4096], P(None, 'ch'), may hold values from -0.5 to 0.5
- dt_bias: float32 [4096], P('ch'), may hold values from -6 to -1
- a_log: float32 [16, 4096], P(None, 'ch'), may hold values from -4 to 2.8
- d_skip: float32 [4096], P('ch'), may hold values from 0.5 to 1.5
- w_out: bfloat16 [3, 2048, 4096], P(None, None, 'ch'), may hold values from -0.1875 to 0.1875
- modes: int32 [2048], replicated, may hold values from 0 to 2
- doc_lengths: int32 [4], replicated, may hold values from 1 to 1024, 2048 in all
- cotangent: bfloat16 [2048, 2048], P('seq', 'ch'), may hold values from -6 to 6
Outputs:
- block_out: bfloat16 [2048, 2048], P('seq', 'ch')
- d_x_in: float32 [2048, 2048], P('seq', 'ch')
- d_norm_gain: float32 [2048], P('ch')
- d_w_in: float32 [3, 2048, 2, 4096], P(None, 'seq', None, 'ch')
- d_conv_weight: float32 [4, 4096], P(None, 'ch')
- d_conv_bias: float32 [4096], P('ch')
- d_x_proj: float32 [4096, 160], P('ch')
- d_dt_proj: float32 [128, 4096], P(None, 'ch')
- d_dt_bias: float32 [4096], P('ch')
- d_a_log: float32 [16, 4096], P(None, 'ch')
- d_d_skip: float32 [4096], P('ch')
- d_w_out: float32 [3, 2048, 4096], P(None, 'seq', 'ch')
Inputs may be any that keep to these rules, and one draw needn't show every extreme that they name: `doc_lengths`: the documents lie end to end in token order and their lengths sum to 2048. `modes`: 0 image, 1 text, 2 speech.
All inputs are finite; a program needn't handle non-finite values.
Results may differ from a plain program's by a relative error of at most 0.012.
Values may be sent and summed in bfloat16 or wider, within the bound.
A program may use at most 192 MiB of HBM per device.

v0:
```python
from functools import partial
import math

import jax
import jax.numpy as jnp
from jax import lax
from jax.sharding import PartitionSpec as P

EPSILON = 1e-05


def from_behind(block, axis, distance):
    devices = range(lax.axis_size(axis))
    route = [(i - distance, i) for i in devices if i - distance in devices]
    return lax.ppermute(block, axis, route)


def carried_in_2(part, axis, combine, identity, reverse):
    count = lax.axis_size(axis)
    place = lax.axis_index(axis)
    ahead = count - 1 - place if reverse else place
    gathered = jax.tree.map(lambda a: lax.all_gather(a, axis), part)
    state = jax.tree.map(lambda a, e: jnp.zeros_like(a) + jnp.asarray(e, a.dtype), part, identity)

    def one(turn, state):
        source = count - 1 - turn if reverse else turn
        return combine(
            state, jax.tree.map(lambda a: lax.dynamic_index_in_dim(a, source, 0, False), gathered)
        )

    return lax.fori_loop(0, ahead, one, state)


def mix_pair(earlier, latter):
    return (earlier[0] * latter[0], latter[0] * earlier[1] + latter[1])


def doc_tables(doc_lengths, positions):
    doc_ends = jnp.cumsum(doc_lengths)
    doc_starts = doc_ends - doc_lengths
    doc_index = jnp.sum((positions[:, None] >= doc_ends[None, :]).astype(jnp.int32), axis=1)
    begins = jnp.any(positions[:, None] == doc_starts[None, :], axis=1)
    return (doc_index, begins)


def to_blocks(array, block_count):
    return array.reshape((block_count, array.shape[0] // block_count) + array.shape[1:])


def run_span(decay_rate, state, span):
    step_c, conv_c, input_c, output_c, keep_c = span
    outputs = []
    for item in range(step_c.shape[0]):
        decay = jnp.exp(step_c[item][None] * decay_rate) * keep_c[item]
        state = decay * state + (step_c[item] * conv_c[item])[None] * input_c[item][:, None]
        outputs.append(jnp.sum(output_c[item][:, None] * state, axis=0))
    return (state, jnp.stack(outputs, axis=0))


def span_scan(decay_rate, carried, spans):

    def advance(state, span):
        end_state, outputs = run_span(decay_rate, state, span)
        return (end_state, (outputs, state))

    return lax.scan(advance, carried, spans)


def span_count(pieces):
    rows = pieces[0].shape[0]
    return rows // math.gcd(16, rows)


def sub_forward(decay_rate, carried, pieces):
    count = span_count(pieces)
    spans = tuple((to_blocks(piece, count) for piece in pieces))
    end_state, (outputs, _) = span_scan(decay_rate, carried, spans)
    return (end_state, (outputs.reshape(-1, outputs.shape[-1]), carried))


def sub_backward(decay_rate, carried, pieces):
    step_piece, conv_piece, input_piece, output_piece, keep_piece, dy_piece, start_state = pieces
    count = span_count(pieces)
    spans = tuple(
        (
            to_blocks(piece, count)
            for piece in (step_piece, conv_piece, input_piece, output_piece, keep_piece, dy_piece)
        )
    )
    _, (_, span_starts) = span_scan(decay_rate, start_state, spans[:5])

    def retreat(carry, item):
        pending, rate_grad = carry
        (step_c, conv_c, input_c, output_c, keep_c, dy_c), state = item
        length = step_c.shape[0]
        decays = []
        befores = []
        states = []
        for index in range(length):
            decay = jnp.exp(step_c[index][None] * decay_rate) * keep_c[index]
            befores.append(state)
            state = decay * state + (step_c[index] * conv_c[index])[None] * input_c[index][:, None]
            decays.append(decay)
            states.append(state)
        step_list = [None] * length
        conv_list = [None] * length
        input_list = [None] * length
        output_list = [None] * length
        for index in reversed(range(length)):
            adjoint = output_c[index][:, None] * dy_c[index][None] + pending
            decay_grad = adjoint * befores[index] * decays[index]
            adj_input = jnp.sum(adjoint * input_c[index][:, None], axis=0)
            step_list[index] = jnp.sum(decay_grad * decay_rate, axis=0) + adj_input * conv_c[index]
            conv_list[index] = adj_input * step_c[index]
            input_list[index] = jnp.sum(adjoint * (step_c[index] * conv_c[index])[None], axis=1)
            output_list[index] = jnp.sum(dy_c[index][None] * states[index], axis=1)
            rate_grad = rate_grad + decay_grad * step_c[index][None]
            pending = decays[index] * adjoint
        return (
            (pending, rate_grad),
            (
                jnp.stack(step_list),
                jnp.stack(conv_list),
                jnp.stack(input_list),
                jnp.stack(output_list),
            ),
        )

    (pending, rate_grad), grads = lax.scan(retreat, carried, (spans, span_starts), reverse=True)
    grads = tuple((grad.reshape((-1,) + grad.shape[2:]) for grad in grads))
    return ((pending, rate_grad), grads)


def shards(
    x_in,
    norm_gain,
    w_in,
    conv_weight,
    conv_bias,
    x_proj,
    dt_proj,
    dt_bias,
    a_log,
    d_skip,
    w_out,
    modes,
    doc_lengths,
    cotangent,
):
    tok_rows, model_width = x_in.shape
    mode_count = w_in.shape[0]
    inner_local = conv_bias.shape[0]
    state_size = a_log.shape[0]
    rank_size = dt_proj.shape[0]
    conv_taps = conv_weight.shape[0]
    ch_count = lax.axis_size("ch")
    feat_part = model_width // ch_count
    seq_index = lax.axis_index("seq")
    ch_index = lax.axis_index("ch")
    first_pos = seq_index * tok_rows
    positions = first_pos + jnp.arange(tok_rows, dtype=jnp.int32)
    my_modes = lax.dynamic_slice_in_dim(modes, first_pos, tok_rows)
    onehot = (my_modes[:, None] == jnp.arange(mode_count, dtype=jnp.int32)[None]).astype(
        jnp.bfloat16
    )
    doc_index, begins = doc_tables(doc_lengths, positions)
    keep_mask = 1.0 - begins.astype(jnp.float32)
    x_full = x_in.astype(jnp.float32)
    scale = lax.rsqrt(jnp.mean(x_full * x_full, axis=1, keepdims=True) + EPSILON)
    normed = (x_full * scale * norm_gain[None]).astype(jnp.bfloat16)
    expanded = (onehot[:, :, None] * normed[:, None, :]).reshape(tok_rows, mode_count * model_width)
    w_in_flat = w_in.reshape(mode_count * model_width, 2 * inner_local)
    projected_xz = jnp.dot(expanded, w_in_flat, preferred_element_type=jnp.float32).astype(
        jnp.bfloat16
    )
    projected_xz = projected_xz.reshape(tok_rows, 2, inner_local)
    x_branch = projected_xz[:, 0]
    z_branch = projected_xz[:, 1].astype(jnp.float32)
    rim_rows = from_behind(x_branch[tok_rows - (conv_taps - 1) :], "seq", 1)
    extended = jnp.concatenate([rim_rows, x_branch], axis=0).astype(jnp.float32)
    ext_doc, _ = doc_tables(
        doc_lengths,
        first_pos - (conv_taps - 1) + jnp.arange(tok_rows + conv_taps - 1, dtype=jnp.int32),
    )
    conv_pre = jnp.zeros((tok_rows, inner_local), jnp.float32) + conv_bias[None]
    same_list = []
    for offset in range(conv_taps):
        same_doc = (ext_doc[offset : offset + tok_rows] == doc_index).astype(jnp.float32)[:, None]
        same_list.append(same_doc)
        conv_pre = (
            conv_pre + conv_weight[offset][None] * extended[offset : offset + tok_rows] * same_doc
        )
    conv_out = jax.nn.silu(conv_pre).astype(jnp.bfloat16)
    conv_float = conv_out.astype(jnp.float32)
    projected = lax.psum(jnp.dot(conv_out, x_proj, preferred_element_type=jnp.float32), "ch")
    dt_low = projected[:, :rank_size].astype(jnp.bfloat16)
    b_in = projected[:, rank_size : rank_size + state_size]
    c_out = projected[:, rank_size + state_size :]
    dt_raw = jnp.dot(dt_low, dt_proj, preferred_element_type=jnp.float32)
    step_size = jax.nn.softplus(dt_raw + dt_bias[None])
    decay_rate = -jnp.exp(a_log)
    block_len = math.gcd(256, tok_rows)
    block_count = tok_rows // block_len
    cum_step = jnp.cumsum(step_size, axis=0)
    alive = ((doc_index == doc_index[0]) & jnp.logical_not(begins[0])).astype(jnp.float32)
    through = jnp.exp(decay_rate * cum_step[-1][None]) * alive[-1]
    reach = jnp.exp(decay_rate[None] * cum_step[:, None, :]) * alive[:, None, None]
    pieces = (
        to_blocks(step_size, block_count),
        to_blocks(conv_float, block_count),
        to_blocks(b_in, block_count),
        to_blocks(c_out, block_count),
        to_blocks(keep_mask, block_count),
    )
    zero_state = jnp.zeros((state_size, inner_local), jnp.float32)
    local_end, (ssm_local, local_starts) = lax.scan(
        partial(sub_forward, decay_rate), zero_state, pieces
    )
    carried_in = carried_in_2(
        (through, local_end), "seq", mix_pair, (jnp.ones_like(through), zero_state), False
    )
    incoming = carried_in[1]
    _, (ssm_blocks, block_starts) = lax.scan(partial(sub_forward, decay_rate), incoming, pieces)
    ssm = ssm_blocks.reshape(tok_rows, inner_local)
    ssm = ssm + d_skip[None] * conv_float
    gate_act = jax.nn.silu(z_branch)
    gated = (ssm * gate_act).astype(jnp.bfloat16)
    proj_all = jnp.einsum("te,mde->tmd", gated, w_out, preferred_element_type=jnp.float32)
    mixer_part = jnp.sum(onehot.astype(jnp.float32)[:, :, None] * proj_all, axis=1)
    mixer = lax.psum_scatter(mixer_part, "ch", scatter_dimension=1, tiled=True)
    x_slice = lax.dynamic_slice_in_dim(x_full, ch_index * feat_part, feat_part, 1)
    block_out = (x_slice + mixer).astype(jnp.bfloat16)
    cot_full = lax.all_gather(cotangent, "ch", axis=1, tiled=True)
    cot_expanded = onehot[:, :, None] * cot_full[:, None, :]
    d_gated = jnp.einsum("tmd,mde->te", cot_expanded, w_out, preferred_element_type=jnp.float32)
    d_ssm = d_gated * gate_act
    gate_sig = jax.nn.sigmoid(z_branch)
    d_z = d_gated * ssm * gate_sig * (1.0 + z_branch * (1.0 - gate_sig))
    d_skip_local = jnp.sum(d_ssm * conv_float, axis=0)
    d_conv = d_ssm * d_skip[None]
    head_sum = jnp.sum(reach * c_out[:, :, None] * d_ssm[:, None, :], axis=0)
    carried_back = carried_in_2(
        (through, head_sum), "seq", mix_pair, (jnp.ones_like(through), zero_state), True
    )
    back_pieces = pieces + (to_blocks(d_ssm, block_count), block_starts)
    (_, rate_grad), (step_grads, conv_grads, input_grads, output_grads) = lax.scan(
        partial(sub_backward, decay_rate), (carried_back[1], zero_state), back_pieces, reverse=True
    )
    d_step = step_grads.reshape(tok_rows, inner_local)
    d_conv = d_conv + conv_grads.reshape(tok_rows, inner_local)
    d_b = input_grads.reshape(tok_rows, state_size)
    d_c = output_grads.reshape(tok_rows, state_size)
    d_a_log = rate_grad * decay_rate
    d_full = d_step * jax.nn.sigmoid(dt_raw + dt_bias[None])
    d_bias_local = jnp.sum(d_full, axis=0)
    d_raw = d_full.astype(jnp.bfloat16)
    d_dt_proj_local = jnp.einsum("tr,te->re", dt_low, d_raw, preferred_element_type=jnp.float32)
    d_low_part = jnp.einsum("te,re->tr", d_raw, dt_proj, preferred_element_type=jnp.float32)
    d_projected = lax.psum(jnp.concatenate([d_low_part, d_b, d_c], axis=1), "ch").astype(
        jnp.bfloat16
    )
    d_x_proj_local = jnp.einsum(
        "te,tk->ek", conv_out, d_projected, preferred_element_type=jnp.float32
    )
    d_conv = d_conv + jnp.einsum(
        "tk,ek->te", d_projected, x_proj, preferred_element_type=jnp.float32
    )
    conv_sig = jax.nn.sigmoid(conv_pre)
    d_pre = d_conv * conv_sig * (1.0 + conv_pre * (1.0 - conv_sig))
    d_conv_bias_local = jnp.sum(d_pre, axis=0)
    d_conv_weight_local = jnp.stack(
        [
            jnp.sum(d_pre * extended[offset : offset + tok_rows] * same_list[offset], axis=0)
            for offset in range(conv_taps)
        ],
        axis=0,
    )
    after_rows = from_behind(d_pre[: conv_taps - 1], "seq", -1)
    d_pre_ext = jnp.concatenate([d_pre, after_rows], axis=0)
    post_doc, _ = doc_tables(
        doc_lengths, first_pos + jnp.arange(tok_rows + conv_taps - 1, dtype=jnp.int32)
    )
    d_x_branch = jnp.zeros((tok_rows, inner_local), jnp.float32)
    for offset in range(conv_taps):
        lag = conv_taps - 1 - offset
        same_doc = (post_doc[lag : lag + tok_rows] == doc_index).astype(jnp.float32)[:, None]
        d_x_branch = (
            d_x_branch + d_pre_ext[lag : lag + tok_rows] * conv_weight[offset][None] * same_doc
        )
    d_both = (
        jnp.stack([d_x_branch, d_z], axis=1).astype(jnp.bfloat16).reshape(tok_rows, 2 * inner_local)
    )
    normed_terms = jnp.einsum(
        "tk,mdk->tmd",
        d_both,
        w_in.reshape(mode_count, model_width, 2 * inner_local),
        preferred_element_type=jnp.float32,
    )
    normed_part = jnp.sum(onehot.astype(jnp.float32)[:, :, None] * normed_terms, axis=1)
    gain_slice = lax.dynamic_slice_in_dim(norm_gain, ch_index * feat_part, feat_part, 0)
    d_normed = lax.psum(normed_part, "ch")
    weighted = d_normed * norm_gain[None]
    mean_term = jnp.mean(weighted * x_full, axis=1, keepdims=True)
    d_slice = lax.dynamic_slice_in_dim(d_normed, ch_index * feat_part, feat_part, 1)
    weighted_slice = d_slice * gain_slice[None]
    d_x_in = cotangent.astype(jnp.float32) + scale * weighted_slice - x_slice * scale**3 * mean_term
    d_gain_part = jnp.sum(d_slice * x_slice * scale, axis=0)
    normed_cols, cot_cols = (
        lax.all_to_all(normed, "seq", split_axis=1, concat_axis=0, tiled=True),
        lax.all_to_all(cot_full, "seq", split_axis=1, concat_axis=0, tiled=True),
    )
    slab = normed_cols.shape[1]
    start_totals = (
        jnp.zeros((mode_count, slab, 2 * inner_local), jnp.float32),
        jnp.zeros((mode_count, slab, inner_local), jnp.float32),
    )
    both_piece = lax.all_gather(d_both, "seq", axis=0, tiled=True)
    gated_piece = lax.all_gather(gated, "seq", axis=0, tiled=True)
    mode_mask = (modes[:, None] == jnp.arange(mode_count, dtype=jnp.int32)[None]).astype(
        jnp.bfloat16
    )
    x_spread = mode_mask[:, :, None] * normed_cols[:, None, :]
    c_spread = mode_mask[:, :, None] * cot_cols[:, None, :]
    acc_in = jnp.einsum("tmd,tk->mdk", x_spread, both_piece, preferred_element_type=jnp.float32)
    d_w_out = start_totals[1] + jnp.einsum(
        "tmd,te->mde", c_spread, gated_piece, preferred_element_type=jnp.float32
    )
    d_w_in = acc_in.reshape(mode_count, slab, 2, inner_local)
    small_sums = lax.psum(
        (
            d_gain_part,
            d_conv_weight_local,
            d_conv_bias_local,
            d_x_proj_local,
            d_dt_proj_local,
            d_bias_local,
            d_a_log,
            d_skip_local,
        ),
        "seq",
    )
    return (
        block_out,
        d_x_in,
        small_sums[0],
        d_w_in,
        small_sums[1],
        small_sums[2],
        small_sums[3],
        small_sums[4],
        small_sums[5],
        small_sums[6],
        small_sums[7],
        d_w_out,
    )


def solution(mesh):
    return jax.shard_map(
        shards,
        mesh=mesh,
        in_specs=(
            P("seq", None),
            P(),
            P(None, None, None, "ch"),
            P(None, "ch"),
            P("ch"),
            P("ch", None),
            P(None, "ch"),
            P("ch"),
            P(None, "ch"),
            P("ch"),
            P(None, None, "ch"),
            P(),
            P(),
            P("seq", "ch"),
        ),
        out_specs=(
            P("seq", "ch"),
            P("seq", "ch"),
            P("ch"),
            P(None, "seq", None, "ch"),
            P(None, "ch"),
            P("ch"),
            P("ch", None),
            P(None, "ch"),
            P("ch"),
            P(None, "ch"),
            P("ch"),
            P(None, "seq", "ch"),
        ),
        check_vma=False,
    )
```

profile of v0, /device:TPU:0, one launch (start us, length us, event | category | flops | bytes accessed | tf_op | source)
XLA Modules:
  0.0 2818.9 jit_solution(10953353448080290986)
XLA Ops:
  13.3 25.6 copy.149
  62.0 12.8 all-gather.7.cloned.1.call-done
  89.2 30.0 %all-reduce.7.cloned.1.call-done = f32[256,160]{0,1:T(8,128)} async-done(((f32[256,160]{0,1:T(8,128)}), f32[256,160]{0,1:T(8,128)}) %all-reduce.7.cloned.1.call-update) | async-done | bytes 163856 | tf_op jit(solution)/shard_map/psum | solution.py:195
  123.9 33.3 %all-gather = f32[128,1024]{1,0:T(8,128)} all-gather(f32[16,1024]{1,0:T(8,128)S(1)} %get-tuple-element.1577), channel_id=2, replica_groups=mesh['seq'=8,'ch'=4] {'seq'}, dimensions={0}, use_global_device_ids=true | all-gather | bytes 589824 | tf_op jit(solution)/shard_map/all_gather | solution.py:22
  159.3 214.7 %while.127 = (s32[]{:T(128)}, f32[16,1024]{1,0:T(8,128)S(1)}, f32[16,16,1024]{2,1,0:T(8,128)S(1)}, f32[16,1024]{1,0:T(8,128)S(1)}, f32[16,16]{1,0:T(8,128)}, /*i...) while((s32[]{:T(128)}, f32[16,1024]{1,0:T(8,128)S(1)}, ...), condition=%wide.region_9.10_spmd.clone, body=%wide.region_8.9_spmd.clone.sunk | while | flops 1343506 | bytes 790367 | solution.py:66
  374.0 33.3 %all-gather.1 = f32[128,1024]{1,0:T(8,128)} all-gather(f32[16,1024]{1,0:T(8,128)S(1)} %get-tuple-element.659), channel_id=3, replica_groups=mesh['seq'=8,'ch'=4] {'seq'}, dimensions={0}, use_global_device_ids=true | all-gather | bytes 589824 | tf_op jit(solution)/shard_map/all_gather | solution.py:22
  408.2 333.5 %while.124 = (s32[]{:T(128)}, f32[16,1024]{1,0:T(8,128)S(1)}, f32[16,16,1024]{2,1,0:T(8,128)S(1)}, f32[16,16,1024]{2,1,0:T(8,128)}, f32[16,1024]{1,0:T(8,128)S(1...) while((s32[]{:T(128)}, f32[16,1024]{1,0:T(8,128)S(1)}, ...), condition=%wide.region_29.30_spmd, body=%wide.region_12.29_spmd.sunk | while | flops 2490385 | bytes 2694537 | solution.py:66
  747.3 39.5 %all-gather.2 = f32[128,1024]{1,0:T(8,128)} all-gather(f32[16,1024]{1,0:T(8,128)S(1)} %multiply_reduce_fusion.80), channel_id=4, replica_groups=mesh['seq'=8,'ch'=4] {'seq'}, dimensions={0}, use_global_device_ids=true | all-gather | bytes 589824 | tf_op jit(solution)/shard_map/all_gather | solution.py:22
  794.9 241.4 %while.126 = (s32[]{:T(128)}, f32[16,1024]{1,0:T(8,128)S(1)}, f32[16,16,1024]{2,1,0:T(8,128)}, f32[16,16,1024]{2,1,0:T(8,128)}, f32[16,1024]{1,0:T(8,128)S(1)}, ...) while((s32[]{:T(128)}, f32[16,1024]{1,0:T(8,128)S(1)}, ...), condition=%wide.region_36.37_spmd, body=%wide.region_35.36_spmd.sunk | while | flops 1327121 | bytes 921441 | solution.py:66
  1039.9 1340.4 %while.128 = (s32[]{:T(128)}, f32[16,1024]{1,0:T(8,128)S(1)}, f32[16,1024]{1,0:T(8,128)}, f32[16,16,1024]{2,1,0:T(8,128)}, f32[16,16,1024]{2,1,0:T(8,128)}, /*in...) while((s32[]{:T(128)}, f32[16,1024]{1,0:T(8,128)S(1)}, ...), condition=%wide.region_102.103_spmd.clone, body=%wide.region_37.102_spmd.clone.sunk | while | flops 9354771 | bytes 7238651 | solution.py:129
  1171.6 12.2 fusion.261
  1255.3 12.2 fusion.261
  1339.1 12.2 fusion.261
  1423.0 12.2 fusion.261
  1506.7 12.2 fusion.261
  1590.4 12.2 fusion.261
  1674.1 12.2 fusion.261
  1758.0 12.2 fusion.261
  1841.8 12.2 fusion.261
  1925.5 12.2 fusion.261
  2009.3 12.2 fusion.261
  2093.2 12.2 fusion.261
  2176.9 12.2 fusion.261
  2260.6 12.2 fusion.261
  2386.1 13.4 all-reduce.12
  2411.1 24.1 fusion.158
  2435.5 15.0 multiply_reduce_fusion.81
  2454.9 26.8 all_to_all.32
  2520.9 38.8 %all-reduce = (f32[512]{0:T(512)}, f32[4,1024]{1,0:T(4,128)}, f32[1024]{0:T(1024)}, f32[1024]{0:T(1024)}, f32[1024]{0:T(1024)}) all-reduce(f32[512]{0:T(512)S(1)} %get-tuple-element.1569, f32[4,1024]{1,0:T(4,128)S(1)} %pad_maximum_fusion.2, f32[1024]{0:T(1024)S(1)} %get-tuple-element.1028, ...), channel_id=1, replica_groups=mesh['seq'=8,'ch'=4] {'seq'}, use_global_device_ids=true, to_apply=%region_109.110 | all-reduce | flops 7680 | bytes 61440 | tf_op jit(solution)/shard_map/psum | solution.py:329
  2559.8 34.8 %all-gather.11.cloned.1.call-done = bf16[2048,1024]{1,0:T(8,128)(2,1)} async-done(((bf16[256,1024]{1,0:T(8,128)(2,1)}), bf16[2048,1024]{1,0:T(8,128)(2,1)}) %all-gather.11.cloned.1.call-update) | async-done | bytes 4194320 | tf_op jit(solution)/shard_map/all_gather | solution.py:318
  2601.8 118.2 %all-gather.9.cloned.1.call-done = bf16[2048,2048]{1,0:T(8,128)(2,1)} async-done(((bf16[256,2048]{1,0:T(8,128)(2,1)}), bf16[2048,2048]{1,0:T(8,128)(2,1)}) %all-gather.9.cloned.1.call-update) | async-done | bytes 8388624 | tf_op jit(solution)/shard_map/all_gather | solution.py:317
  2739.8 66.7 %all-reduce.11.cloned.1.call-done = (f32[1024,160]{0,1:T(8,128)}, f32[128,1024]{1,0:T(8,128)}, f32[16,1024]{1,0:T(8,128)}) async-done(((f32[1024,160]{0,1:T(8,128)}, f32[128,1024]{1,0:T(8,128)}, f32[16,1024]{1,0:T(8,128)}), (f32[1024,160]{0,1:T(8,128)}, f32[128,1024]{1,0:T(8,128)}, f32[16,1024]{1,0:T(8,128)})) %all-reduce.11.cloned.1.call-update) | async-done | bytes 1245200 | tf_op jit(solution)/shard_map/psum | solution.py:329
  (4785 shorter events, 2099.2 us)
Async XLA Ops:
  7.2 79.3 %copy-start = (bf16[1024,160]{0,1:T(8,128)(2,1)S(1)}, bf16[1024,160]{0,1:T(8,128)(2,1)}, u32[]{:S(2)}) copy-start(bf16[1024,160]{0,1:T(8,128)(2,1)} %param.31) | copy-start | bytes 983044
  7.2 67.6 %all-gather.7.cloned.1.call-start = ((), (), s32[]{:S(2)}) async-start(), calls=%async_computation.5 | async-start | bytes 1310720 | tf_op jit(solution)/shard_map/all_gather | solution.py:233
  51.9 9.9 collective-permute-start
  57.6 61.6 %all-reduce.7.cloned.1.call-start = ((), (), s32[]{:S(2)}) async-start(), calls=%async_computation.3 | async-start | bytes 327680 | tf_op jit(solution)/shard_map/psum | solution.py:195
  87.5 2408.7 %all-reduce.9.cloned.1.call-start = ((), (), s32[]{:S(2)}) async-start(), calls=%async_computation.6 | async-start | bytes 4194304 | tf_op jit(solution)/shard_map/psum | solution.py:301
  1146.1 55.5 %copy-start.25 = (f32[1,1,1024]{2,1,0:T(1,128)S(1)}, f32[1,1,1024]{2,1,0:T(1,128)}, u32[]{:S(2)}) copy-start(f32[1,1,1024]{2,1,0:T(1,128)} %copy-done.24) | copy-start | bytes 12292 | tf_op jit(solution)/shard_map/while/body/eval_jaxpr/while
  1146.1 55.5 %copy-start.60 = (f32[1,1,1024]{2,1,0:T(1,128)S(1)}, f32[1,1,1024]{2,1,0:T(1,128)}, u32[]{:S(2)}) copy-start(f32[1,1,1024]{2,1,0:T(1,128)} %get-tuple-element.2607) | copy-start | bytes 12292 | tf_op jit(solution)/shard_map/while/body/eval_jaxpr/while
  1229.8 55.5 %copy-start.25 = (f32[1,1,1024]{2,1,0:T(1,128)S(1)}, f32[1,1,1024]{2,1,0:T(1,128)}, u32[]{:S(2)}) copy-start(f32[1,1,1024]{2,1,0:T(1,128)} %copy-done.24) | copy-start | bytes 12292 | tf_op jit(solution)/shard_map/while/body/eval_jaxpr/while
  1229.8 55.5 %copy-start.60 = (f32[1,1,1024]{2,1,0:T(1,128)S(1)}, f32[1,1,1024]{2,1,0:T(1,128)}, u32[]{:S(2)}) copy-start(f32[1,1,1024]{2,1,0:T(1,128)} %get-tuple-element.2607) | copy-start | bytes 12292 | tf_op jit(solution)/shard_map/while/body/eval_jaxpr/while
  1313.5 55.5 %copy-start.25 = (f32[1,1,1024]{2,1,0:T(1,128)S(1)}, f32[1,1,1024]{2,1,0:T(1,128)}, u32[]{:S(2)}) copy-start(f32[1,1,1024]{2,1,0:T(1,128)} %copy-done.24) | copy-start | bytes 12292 | tf_op jit(solution)/shard_map/while/body/eval_jaxpr/while
  1313.6 55.5 %copy-start.60 = (f32[1,1,1024]{2,1,0:T(1,128)S(1)}, f32[1,1,1024]{2,1,0:T(1,128)}, u32[]{:S(2)}) copy-start(f32[1,1,1024]{2,1,0:T(1,128)} %get-tuple-element.2607) | copy-start | bytes 12292 | tf_op jit(solution)/shard_map/while/body/eval_jaxpr/while
  1397.4 55.5 %copy-start.25 = (f32[1,1,1024]{2,1,0:T(1,128)S(1)}, f32[1,1,1024]{2,1,0:T(1,128)}, u32[]{:S(2)}) copy-start(f32[1,1,1024]{2,1,0:T(1,128)} %copy-done.24) | copy-start | bytes 12292 | tf_op jit(solution)/shard_map/while/body/eval_jaxpr/while
  1397.5 55.5 %copy-start.60 = (f32[1,1,1024]{2,1,0:T(1,128)S(1)}, f32[1,1,1024]{2,1,0:T(1,128)}, u32[]{:S(2)}) copy-start(f32[1,1,1024]{2,1,0:T(1,128)} %get-tuple-element.2607) | copy-start | bytes 12292 | tf_op jit(solution)/shard_map/while/body/eval_jaxpr/while
  1481.2 55.5 %copy-start.25 = (f32[1,1,1024]{2,1,0:T(1,128)S(1)}, f32[1,1,1024]{2,1,0:T(1,128)}, u32[]{:S(2)}) copy-start(f32[1,1,1024]{2,1,0:T(1,128)} %copy-done.24) | copy-start | bytes 12292 | tf_op jit(solution)/shard_map/while/body/eval_jaxpr/while
  1481.2 55.5 %copy-start.60 = (f32[1,1,1024]{2,1,0:T(1,128)S(1)}, f32[1,1,1024]{2,1,0:T(1,128)}, u32[]{:S(2)}) copy-start(f32[1,1,1024]{2,1,0:T(1,128)} %get-tuple-element.2607) | copy-start | bytes 12292 | tf_op jit(solution)/shard_map/while/body/eval_jaxpr/while
  1564.9 55.5 %copy-start.25 = (f32[1,1,1024]{2,1,0:T(1,128)S(1)}, f32[1,1,1024]{2,1,0:T(1,128)}, u32[]{:S(2)}) copy-start(f32[1,1,1024]{2,1,0:T(1,128)} %copy-done.24) | copy-start | bytes 12292 | tf_op jit(solution)/shard_map/while/body/eval_jaxpr/while
  1564.9 55.5 %copy-start.60 = (f32[1,1,1024]{2,1,0:T(1,128)S(1)}, f32[1,1,1024]{2,1,0:T(1,128)}, u32[]{:S(2)}) copy-start(f32[1,1,1024]{2,1,0:T(1,128)} %get-tuple-element.2607) | copy-start | bytes 12292 | tf_op jit(solution)/shard_map/while/body/eval_jaxpr/while
  1648.6 55.5 %copy-start.25 = (f32[1,1,1024]{2,1,0:T(1,128)S(1)}, f32[1,1,1024]{2,1,0:T(1,128)}, u32[]{:S(2)}) copy-start(f32[1,1,1024]{2,1,0:T(1,128)} %copy-done.24) | copy-start | bytes 12292 | tf_op jit(solution)/shard_map/while/body/eval_jaxpr/while
  1648.6 55.5 %copy-start.60 = (f32[1,1,1024]{2,1,0:T(1,128)S(1)}, f32[1,1,1024]{2,1,0:T(1,128)}, u32[]{:S(2)}) copy-start(f32[1,1,1024]{2,1,0:T(1,128)} %get-tuple-element.2607) | copy-start | bytes 12292 | tf_op jit(solution)/shard_map/while/body/eval_jaxpr/while
  1732.5 55.5 %copy-start.25 = (f32[1,1,1024]{2,1,0:T(1,128)S(1)}, f32[1,1,1024]{2,1,0:T(1,128)}, u32[]{:S(2)}) copy-start(f32[1,1,1024]{2,1,0:T(1,128)} %copy-done.24) | copy-start | bytes 12292 | tf_op jit(solution)/shard_map/while/body/eval_jaxpr/while
  1732.5 55.5 %copy-start.60 = (f32[1,1,1024]{2,1,0:T(1,128)S(1)}, f32[1,1,1024]{2,1,0:T(1,128)}, u32[]{:S(2)}) copy-start(f32[1,1,1024]{2,1,0:T(1,128)} %get-tuple-element.2607) | copy-start | bytes 12292 | tf_op jit(solution)/shard_map/while/body/eval_jaxpr/while
  1816.3 55.5 %copy-start.25 = (f32[1,1,1024]{2,1,0:T(1,128)S(1)}, f32[1,1,1024]{2,1,0:T(1,128)}, u32[]{:S(2)}) copy-start(f32[1,1,1024]{2,1,0:T(1,128)} %copy-done.24) | copy-start | bytes 12292 | tf_op jit(solution)/shard_map/while/body/eval_jaxpr/while
  1816.3 55.5 %copy-start.60 = (f32[1,1,1024]{2,1,0:T(1,128)S(1)}, f32[1,1,1024]{2,1,0:T(1,128)}, u32[]{:S(2)}) copy-start(f32[1,1,1024]{2,1,0:T(1,128)} %get-tuple-element.2607) | copy-start | bytes 12292 | tf_op jit(solution)/shard_map/while/body/eval_jaxpr/while
  2404.7 5.6 collective-permute-start.1
  2435.2 83.2 %reduce-scatter.2.cloned.1.call-start = ((), (), s32[]{:S(2)}) async-start(), calls=%async_computation.4 | async-start | bytes 2621440 | tf_op jit(solution)/shard_map/reduce_scatter | solution.py:230
  2450.5 144.0 %all-gather.11.cloned.1.call-start = ((), (), s32[]{:S(2)}) async-start(), calls=%async_computation.8 | async-start | bytes 4718592 | tf_op jit(solution)/shard_map/all_gather | solution.py:318
  2451.1 268.8 %all-gather.9.cloned.1.call-start = ((), (), s32[]{:S(2)}) async-start(), calls=%async_computation.7 | async-start | bytes 9437184 | tf_op jit(solution)/shard_map/all_gather | solution.py:317
  2481.8 28.5 %all-to-all-start.1 = ((bf16[256,8,256]{0,2,1:T(8,128)(2,1)}), bf16[256,8,256]{0,2,1:T(8,128)(2,1)S(1)}, u32[]{:S(2)}, u32[]{:S(2)}) async-start(bf16[256,8,256]{0,2,1:T(8,128)(2,1)} %bitcast.1538), calls=%async_computation.2 | async-start | bytes 2097152 | tf_op jit(solution)/shard_map/all_to_all | solution.py:310
  2485.5 321.0 %all-reduce.11.cloned.1.call-start = ((), (), s32[]{:S(2)}) async-start(), calls=%async_computation.9 | async-start | bytes 2490368 | tf_op jit(solution)/shard_map/psum | solution.py:329
  2510.2 84.3 %copy-start.111 = (bf16[2048,3]{0,1:T(4,128)(2,1)S(1)}, bf16[2048,3]{0,1:T(4,128)(2,1)}, u32[]{:S(2)}) copy-start(bf16[2048,3]{0,1:T(4,128)(2,1)} %fusion.212) | copy-start | bytes 36868
  2559.8 160.2 %copy-start.46 = (bf16[2048,256]{0,1:T(8,128)(2,1)S(1)}, bf16[2048,256]{0,1:T(8,128)(2,1)}, u32[]{:S(2)}) copy-start(bf16[2048,256]{0,1:T(8,128)(2,1)} %copy.135) | copy-start | bytes 3145732
  2730.6 81.2 %copy-start.1 = (bf16[1024,160]{0,1:T(8,128)(2,1)S(1)}, bf16[1024,160]{0,1:T(8,128)(2,1)}, u32[]{:S(2)}) copy-start(bf16[1024,160]{0,1:T(8,128)(2,1)} %param.31) | copy-start | bytes 983044
  (1269 other events, 38372.8 us)
Sparse Core Ops, SparseCore 0:
  57.7 17.0 all-gather.6
  87.6 31.5 all-reduce.6
  2435.3 49.1 all-reduce.8
  2486.9 31.4 reduce-scatter.1
  2520.7 73.8 all-gather.10
  2596.7 123.1 all-gather.8
  2725.4 81.0 all-reduce.10
where the time goes:
time: 2870 us; the launch traced here: 2820 us
  other arithmetic  1710 us (60%)
  local copies, waits for them, and re-layouts  492 us (17%)
  waiting for transfers between devices  285 us (10%)
  blocking collectives  185 us (6%)
  matrix products  89.2 us (3%)
    add x32, other arithmetic, run_span(): decay * state + (step_c[item] * conv_c[item])[None] * input_c[item][:, None]  333 us
    reduce_sum x112, other arithmetic, retreat(): jnp.sum(decay_grad * decay_rate, axis=0) + adj_input * conv_c[index]  313 us
    reduce_sum x112, other arithmetic, run_span(): outputs.append(jnp.sum(output_c[item][:, None] * state, axis=0))  260 us
    add x16, other arithmetic, retreat(): rate_grad = rate_grad + decay_grad * step_c[index][None]  195 us
    reduce_sum x16, other arithmetic, retreat(): output_list[index] = jnp.sum(dy_c[index][None] * states[index], axis=1)  192 us
    mul x256, other arithmetic, retreat(): step_c[index] * conv_c[index]  155 us
    all_gather x1, waiting for transfers between devices, shards(): both_piece = lax.all_gather(d_both, 'seq', axis=0, tiled=True)  118 us
    reduce_sum x32, other arithmetic, retreat(): jnp.sum(adjoint * (step_c[index] * conv_c[index])[None], axis=1)  115 us

commit v1 on v0

v1 whole, which is shorter than its diff:
```python
import functools
import math

import jax
import jax.numpy as jnp
from jax import lax
from jax.experimental import pallas as pl
from jax.experimental.pallas import tpu as pltpu
from jax.sharding import PartitionSpec as P

EPSILON = 1e-05


def from_behind(block, axis, distance):
    devices = range(lax.axis_size(axis))
    route = [(i - distance, i) for i in devices if i - distance in devices]
    return lax.ppermute(block, axis, route)


def doc_tables(doc_lengths, positions):
    count = doc_lengths.shape[0]
    order = jnp.arange(count, dtype=jnp.int32)
    doc_ends = jnp.sum(jnp.where(order[:, None] >= order[None, :], doc_lengths[None, :], 0), axis=1)
    doc_starts = doc_ends - doc_lengths
    doc_index = jnp.sum((positions[:, None] >= doc_ends[None, :]).astype(jnp.int32), axis=1)
    begins = jnp.any(positions[:, None] == doc_starts[None, :], axis=1)
    return (doc_index, begins)


def own_columns(values):
    rows, n = values.shape
    own = jnp.arange(16 * n)[None] // n == jnp.arange(rows)[:, None] % 16
    return jnp.where(own, jnp.tile(values, (1, 16)), 0).astype(jnp.bfloat16)


LB = 512
CH = 32
NS = 16

def tile_lanes(v, lanes):
    return jnp.concatenate([v] * (lanes // 128), axis=1)

def ends_kernel(lb, dtd_ref, u_ref, g_ref, b_ref, c_ref, rate_ref, out_ref):
    n = rate_ref.shape[0]
    rows, chans = dtd_ref.shape
    @pl.when(pl.program_id(0) == 0)
    def _():
        out_ref[0:n, :] = jnp.zeros((n, chans), jnp.float32)
        out_ref[n:2*n, :] = jnp.ones((n, chans), jnp.float32)
        out_ref[2*n:3*n, :] = jnp.zeros((n, chans), jnp.float32)
    for block in range(chans // lb):
        cut = slice(block * lb, (block + 1) * lb)
        rate = rate_ref[:, cut]
        h = out_ref[0:n, cut]
        reach = out_ref[n:2*n, cut]
        head = out_ref[2*n:3*n, cut]
        for t in range(rows):
            decay = jnp.exp2(dtd_ref[t:t+1, cut] * rate)
            h = decay * h + u_ref[t:t+1, cut] * tile_lanes(b_ref[t], lb)
            reach = reach * decay
            head = head + reach * (g_ref[t:t+1, cut] * tile_lanes(c_ref[t], lb))
        out_ref[0:n, cut] = h
        out_ref[n:2*n, cut] = reach
        out_ref[2*n:3*n, cut] = head

def scan_ends(dtd, u, g, b, c, rate, lb=LB, ch=CH):
    t, e = dtd.shape
    n = rate.shape[0]
    row = pl.BlockSpec((ch, e), lambda i: (i, 0))
    wide = pl.BlockSpec((ch, n, 128), lambda i: (i, 0, 0))
    return pl.pallas_call(
        functools.partial(ends_kernel, lb),
        grid=(t // ch,),
        in_specs=[row, row, row, wide, wide, pl.BlockSpec((n, e), lambda i: (0, 0))],
        out_specs=pl.BlockSpec((3 * n, e), lambda i: (0, 0)),
        out_shape=jax.ShapeDtypeStruct((3 * n, e), jnp.float32),
        compiler_params=pltpu.CompilerParams(vmem_limit_bytes=32 << 20),
        name="scan_ends",
    )(dtd, u, g, b, c, rate)

def forward_kernel(lb, dtd_ref, u_ref, b_ref, cblk_ref, rate_ref, h0_ref, y_ref, hist_ref, state_ref):
    n = rate_ref.shape[0]
    rows, chans = dtd_ref.shape
    @pl.when(pl.program_id(0) == 0)
    def _():
        state_ref[...] = h0_ref[...]
    for block in range(chans // lb):
        cut = slice(block * lb, (block + 1) * lb)
        rate = rate_ref[:, cut]
        h = state_ref[:, cut]
        for t in range(rows):
            decay = jnp.exp2(dtd_ref[t:t+1, cut] * rate)
            h = decay * h + u_ref[t:t+1, cut] * tile_lanes(b_ref[t], lb)
            hist_ref[t * n:(t + 1) * n, cut] = h.astype(jnp.bfloat16)
        state_ref[:, cut] = h
    for k in range(rows // 16):
        y_ref[k*16:(k+1)*16, :] = jnp.dot(cblk_ref[k*16:(k+1)*16, :], hist_ref[k*16*n:(k+1)*16*n, :], preferred_element_type=jnp.float32)

def scan_forward(dtd, u, b, cblk, rate, h0, lb=LB, ch=CH):
    t, e = dtd.shape
    n = rate.shape[0]
    row = pl.BlockSpec((ch, e), lambda i: (i, 0))
    wide = pl.BlockSpec((ch, n, 128), lambda i: (i, 0, 0))
    whole = pl.BlockSpec((n, e), lambda i: (0, 0))
    return pl.pallas_call(
        functools.partial(forward_kernel, lb),
        grid=(t // ch,),
        in_specs=[row, row, wide, pl.BlockSpec((ch, 16 * n), lambda i: (i, 0)), whole, whole],
        out_specs=(row, pl.BlockSpec((ch * n, e), lambda i: (i, 0))),
        out_shape=(jax.ShapeDtypeStruct((t, e), jnp.float32), jax.ShapeDtypeStruct((t * n, e), jnp.bfloat16)),
        scratch_shapes=[pltpu.VMEM((n, e), jnp.float32)],
        compiler_params=pltpu.CompilerParams(vmem_limit_bytes=32 << 20),
        name="scan_forward",
    )(dtd, u, b, cblk, rate, h0)

def backward_kernel(lb, dtd_ref, step_ref, conv_ref, g_ref, c_ref, bblk_ref, rate_ref, lam0_ref, h0_ref, hist_ref, prev_ref,
                    gstep_ref, gscan_ref, gb_ref, gc_ref, racc_ref, pend_ref, lam_ref, w_ref):
    n = rate_ref.shape[0]
    rows, chans = dtd_ref.shape
    last = pl.num_programs(0) - 1
    @pl.when(pl.program_id(0) == 0)
    def _():
        pend_ref[...] = lam0_ref[...]
        racc_ref[...] = jnp.zeros_like(racc_ref)
    first = pl.program_id(0) == last
    for block in range(chans // lb):
        cut = slice(block * lb, (block + 1) * lb)
        rate = rate_ref[:, cut]
        pend = pend_ref[:, cut]
        racc = racc_ref[:, cut]
        for t in reversed(range(rows)):
            decay = jnp.exp2(dtd_ref[t:t+1, cut] * rate)
            lam = g_ref[t:t+1, cut] * tile_lanes(c_ref[t], lb) + pend
            pend = decay * lam
            if t:
                before = hist_ref[(t - 1) * n:t * n, cut].astype(jnp.float32)
            else:
                before = jnp.where(first, h0_ref[:, cut], prev_ref[:, cut].astype(jnp.float32))
            w = pend * before
            racc = racc + w * step_ref[t:t+1, cut]
            lam_ref[t * n:(t + 1) * n, cut] = lam.astype(jnp.bfloat16)
            w_ref[t * n:(t + 1) * n, cut] = (w * rate).astype(jnp.bfloat16)
        pend_ref[:, cut] = pend
        racc_ref[:, cut] = racc
    for k in range(rows // 16):
        rc = slice(k * 16, (k + 1) * 16)
        hc = slice(k * 16 * n, (k + 1) * 16 * n)
        step = step_ref[rc, :]
        conv = conv_ref[rc, :]
        own = (lax.broadcasted_iota(jnp.int32, (16, 16 * n), 1) // n == lax.broadcasted_iota(jnp.int32, (16, 16 * n), 0))
        ones = own.astype(jnp.bfloat16)
        adj = jnp.dot(bblk_ref[rc, :], lam_ref[hc, :], preferred_element_type=jnp.float32)
        wsum = jnp.dot(ones, w_ref[hc, :], preferred_element_type=jnp.float32)
        gstep_ref[rc, :] = wsum * math.log(2.0) + adj * conv
        gscan_ref[rc, :] = adj * step
        nt = (((1,), (1,)), ((), ()))
        gb = lax.dot_general((step * conv).astype(jnp.bfloat16), lam_ref[hc, :], nt, preferred_element_type=jnp.float32)
        gc = lax.dot_general(g_ref[rc, :].astype(jnp.bfloat16), hist_ref[hc, :], nt, preferred_element_type=jnp.float32)
        gb_ref[k:k+1] = jnp.sum(jnp.where(own, gb, 0.0), axis=0, keepdims=True)[None]
        gc_ref[k:k+1] = jnp.sum(jnp.where(own, gc, 0.0), axis=0, keepdims=True)[None]

def scan_backward(dtd, step, conv, g, c, bblk, rate, lam0, h0, hist, lb=LB, ch=CH):
    t, e = dtd.shape
    n = rate.shape[0]
    k = t // ch
    row = pl.BlockSpec((ch, e), lambda i: (k - 1 - i, 0))
    wide = pl.BlockSpec((ch, n, 128), lambda i: (k - 1 - i, 0, 0))
    whole = pl.BlockSpec((n, e), lambda i: (0, 0))
    flat = pl.BlockSpec((ch // 16, 1, 16 * n), lambda i: (k - 1 - i, 0, 0))
    outs = pl.pallas_call(
        functools.partial(backward_kernel, lb),
        grid=(k,),
        in_specs=[row, row, row, row, wide, pl.BlockSpec((ch, 16 * n), lambda i: (k - 1 - i, 0)), whole, whole, whole,
                  pl.BlockSpec((ch * n, e), lambda i: (k - 1 - i, 0)),
                  pl.BlockSpec((n, e), lambda i: (jnp.maximum((k - 1 - i) * ch - 1, 0), 0))],
        out_specs=(row, row, flat, flat, whole),
        out_shape=(jax.ShapeDtypeStruct((t, e), jnp.float32), jax.ShapeDtypeStruct((t, e), jnp.float32),
                   jax.ShapeDtypeStruct((t // 16, 1, 16 * n), jnp.float32), jax.ShapeDtypeStruct((t // 16, 1, 16 * n), jnp.float32),
                   jax.ShapeDtypeStruct((n, e), jnp.float32)),
        scratch_shapes=[pltpu.VMEM((n, e), jnp.float32), pltpu.VMEM((ch * n, e), jnp.bfloat16), pltpu.VMEM((ch * n, e), jnp.bfloat16)],
        compiler_params=pltpu.CompilerParams(vmem_limit_bytes=48 << 20),
        name="scan_backward",
    )(dtd, step, conv, g, c, bblk, rate, lam0, h0, hist, hist)
    return outs[0], outs[1], outs[2].reshape(t, n), outs[3].reshape(t, n), outs[4]


def shards(
    x_in,
    norm_gain,
    w_in,
    conv_weight,
    conv_bias,
    x_proj,
    dt_proj,
    dt_bias,
    a_log,
    d_skip,
    w_out,
    modes,
    doc_lengths,
    cotangent,
):
    tok_rows, model_width = x_in.shape
    mode_count = w_in.shape[0]
    inner_local = conv_bias.shape[0]
    state_size = a_log.shape[0]
    rank_size = dt_proj.shape[0]
    conv_taps = conv_weight.shape[0]
    ch_count = lax.axis_size("ch")
    feat_part = model_width // ch_count
    seq_index = lax.axis_index("seq")
    ch_index = lax.axis_index("ch")
    first_pos = seq_index * tok_rows
    positions = first_pos + jnp.arange(tok_rows, dtype=jnp.int32)
    my_modes = lax.dynamic_slice_in_dim(modes, first_pos, tok_rows)
    onehot = (my_modes[:, None] == jnp.arange(mode_count, dtype=jnp.int32)[None]).astype(
        jnp.bfloat16
    )
    doc_index, begins = doc_tables(doc_lengths, positions)
    keep_mask = 1.0 - begins.astype(jnp.float32)
    x_full = x_in.astype(jnp.float32)
    scale = lax.rsqrt(jnp.mean(x_full * x_full, axis=1, keepdims=True) + EPSILON)
    normed = (x_full * scale * norm_gain[None]).astype(jnp.bfloat16)
    expanded = (onehot[:, :, None] * normed[:, None, :]).reshape(tok_rows, mode_count * model_width)
    w_in_flat = w_in.reshape(mode_count * model_width, 2 * inner_local)
    projected_xz = jnp.dot(expanded, w_in_flat, preferred_element_type=jnp.float32).astype(
        jnp.bfloat16
    )
    projected_xz = projected_xz.reshape(tok_rows, 2, inner_local)
    x_branch = projected_xz[:, 0]
    z_branch = projected_xz[:, 1].astype(jnp.float32)
    rim_rows = from_behind(x_branch[tok_rows - (conv_taps - 1) :], "seq", 1)
    extended = jnp.concatenate([rim_rows, x_branch], axis=0).astype(jnp.float32)
    ext_doc, _ = doc_tables(
        doc_lengths,
        first_pos - (conv_taps - 1) + jnp.arange(tok_rows + conv_taps - 1, dtype=jnp.int32),
    )
    conv_pre = jnp.zeros((tok_rows, inner_local), jnp.float32) + conv_bias[None]
    same_list = []
    for offset in range(conv_taps):
        same_doc = (ext_doc[offset : offset + tok_rows] == doc_index).astype(jnp.float32)[:, None]
        same_list.append(same_doc)
        conv_pre = (
            conv_pre + conv_weight[offset][None] * extended[offset : offset + tok_rows] * same_doc
        )
    conv_out = jax.nn.silu(conv_pre).astype(jnp.bfloat16)
    conv_float = conv_out.astype(jnp.float32)
    projected = lax.psum(jnp.dot(conv_out, x_proj, preferred_element_type=jnp.float32), "ch")
    dt_low = projected[:, :rank_size].astype(jnp.bfloat16)
    b_in = projected[:, rank_size : rank_size + state_size]
    c_out = projected[:, rank_size + state_size :]
    dt_raw = jnp.dot(dt_low, dt_proj, preferred_element_type=jnp.float32)
    step_size = jax.nn.softplus(dt_raw + dt_bias[None])
    decay_rate = -jnp.exp(a_log)
    seq_count = lax.axis_size("seq")
    rate_two = decay_rate * math.log2(math.e)
    masked_step = jnp.where(begins[:, None], 1e30, step_size)
    drive = step_size * conv_float
    wide = (tok_rows, state_size, 128)
    b_wide = jnp.broadcast_to(b_in[:, :, None], wide)
    c_wide = jnp.broadcast_to(c_out[:, :, None], wide)
    gate_act = jax.nn.silu(z_branch)
    cot_full = lax.all_gather(cotangent, "ch", axis=1, tiled=True)
    cot_expanded = onehot[:, :, None] * cot_full[:, None, :]
    d_gated = jnp.einsum("tmd,mde->te", cot_expanded, w_out, preferred_element_type=jnp.float32)
    d_ssm = d_gated * gate_act
    ends = lax.all_gather(
        scan_ends(masked_step, drive, d_ssm, b_wide, c_wide, rate_two), "seq", axis=0
    )
    incoming = jnp.zeros((state_size, inner_local), jnp.float32)
    pending = incoming
    for place in range(seq_count):
        part = ends[place]
        after = part[state_size : 2 * state_size] * incoming + part[:state_size]
        incoming = jnp.where(place < seq_index, after, incoming)
    for place in reversed(range(seq_count)):
        part = ends[place]
        after = part[state_size : 2 * state_size] * pending + part[2 * state_size :]
        pending = jnp.where(place > seq_index, after, pending)
    ssm, history = scan_forward(
        masked_step, drive, b_wide, own_columns(c_out), rate_two, incoming
    )
    ssm = ssm + d_skip[None] * conv_float
    gated = (ssm * gate_act).astype(jnp.bfloat16)
    proj_all = jnp.einsum("te,mde->tmd", gated, w_out, preferred_element_type=jnp.float32)
    mixer_part = jnp.sum(onehot.astype(jnp.float32)[:, :, None] * proj_all, axis=1)
    mixer = lax.psum_scatter(mixer_part, "ch", scatter_dimension=1, tiled=True)
    x_slice = lax.dynamic_slice_in_dim(x_full, ch_index * feat_part, feat_part, 1)
    block_out = (x_slice + mixer).astype(jnp.bfloat16)
    gate_sig = jax.nn.sigmoid(z_branch)
    d_z = d_gated * ssm * gate_sig * (1.0 + z_branch * (1.0 - gate_sig))
    d_z = d_z.astype(jnp.bfloat16)
    gated_all = lax.all_gather(gated, "seq", axis=0, tiled=True)
    d_z_all = lax.all_gather(d_z, "seq", axis=0, tiled=True)
    d_skip_local = jnp.sum(d_ssm * conv_float, axis=0)
    d_conv = d_ssm * d_skip[None]
    d_step, conv_grads, d_b, d_c, rate_grad = scan_backward(
        masked_step, step_size, conv_float, d_ssm, c_wide, own_columns(b_in), rate_two, pending, incoming, history
    )
    d_conv = d_conv + conv_grads
    d_a_log = rate_grad * decay_rate
    d_full = d_step * jax.nn.sigmoid(dt_raw + dt_bias[None])
    d_bias_local = jnp.sum(d_full, axis=0)
    d_raw = d_full.astype(jnp.bfloat16)
    d_dt_proj_local = jnp.einsum("tr,te->re", dt_low, d_raw, preferred_element_type=jnp.float32)
    d_low_part = jnp.einsum("te,re->tr", d_raw, dt_proj, preferred_element_type=jnp.float32)
    d_projected = lax.psum(jnp.concatenate([d_low_part, d_b, d_c], axis=1), "ch").astype(
        jnp.bfloat16
    )
    d_x_proj_local = jnp.einsum(
        "te,tk->ek", conv_out, d_projected, preferred_element_type=jnp.float32
    )
    d_conv = d_conv + jnp.einsum(
        "tk,ek->te", d_projected, x_proj, preferred_element_type=jnp.float32
    )
    conv_sig = jax.nn.sigmoid(conv_pre)
    d_pre = d_conv * conv_sig * (1.0 + conv_pre * (1.0 - conv_sig))
    d_conv_bias_local = jnp.sum(d_pre, axis=0)
    d_conv_weight_local = jnp.stack(
        [
            jnp.sum(d_pre * extended[offset : offset + tok_rows] * same_list[offset], axis=0)
            for offset in range(conv_taps)
        ],
        axis=0,
    )
    after_rows = from_behind(d_pre[: conv_taps - 1], "seq", -1)
    d_pre_ext = jnp.concatenate([d_pre, after_rows], axis=0)
    post_doc, _ = doc_tables(
        doc_lengths, first_pos + jnp.arange(tok_rows + conv_taps - 1, dtype=jnp.int32)
    )
    d_x_branch = jnp.zeros((tok_rows, inner_local), jnp.float32)
    for offset in range(conv_taps):
        lag = conv_taps - 1 - offset
        same_doc = (post_doc[lag : lag + tok_rows] == doc_index).astype(jnp.float32)[:, None]
        d_x_branch = (
            d_x_branch + d_pre_ext[lag : lag + tok_rows] * conv_weight[offset][None] * same_doc
        )
    d_x_branch = d_x_branch.astype(jnp.bfloat16)
    d_x_all = lax.all_gather(d_x_branch, "seq", axis=0, tiled=True)
    d_both = jnp.stack([d_x_branch, d_z], axis=1).reshape(tok_rows, 2 * inner_local)
    normed_terms = jnp.einsum(
        "tk,mdk->tmd",
        d_both,
        w_in.reshape(mode_count, model_width, 2 * inner_local),
        preferred_element_type=jnp.float32,
    )
    normed_part = jnp.sum(onehot.astype(jnp.float32)[:, :, None] * normed_terms, axis=1)
    gain_slice = lax.dynamic_slice_in_dim(norm_gain, ch_index * feat_part, feat_part, 0)
    d_normed = lax.psum(normed_part, "ch")
    weighted = d_normed * norm_gain[None]
    mean_term = jnp.mean(weighted * x_full, axis=1, keepdims=True)
    d_slice = lax.dynamic_slice_in_dim(d_normed, ch_index * feat_part, feat_part, 1)
    weighted_slice = d_slice * gain_slice[None]
    d_x_in = cotangent.astype(jnp.float32) + scale * weighted_slice - x_slice * scale**3 * mean_term
    d_gain_part = jnp.sum(d_slice * x_slice * scale, axis=0)
    pair = jnp.concatenate(
        [normed.reshape(tok_rows, seq_count, -1), cot_full.reshape(tok_rows, seq_count, -1)], axis=2
    ).reshape(tok_rows, -1)
    pair_cols = lax.all_to_all(pair, "seq", split_axis=1, concat_axis=0, tiled=True)
    slab = pair_cols.shape[1] // 2
    mode_mask = (modes[:, None] == jnp.arange(mode_count, dtype=jnp.int32)[None]).astype(
        jnp.bfloat16
    )
    x_spread = mode_mask[:, :, None] * pair_cols[:, None, :slab]
    c_spread = mode_mask[:, :, None] * pair_cols[:, None, slab:]
    d_w_out = jnp.einsum("tmd,te->mde", c_spread, gated_all, preferred_element_type=jnp.float32)
    d_w_z = jnp.einsum("tmd,te->mde", x_spread, d_z_all, preferred_element_type=jnp.float32)
    d_w_x = jnp.einsum("tmd,te->mde", x_spread, d_x_all, preferred_element_type=jnp.float32)
    d_w_in = jnp.stack([d_w_x, d_w_z], axis=2)
    small_sums = lax.psum(
        (
            d_gain_part,
            d_conv_weight_local,
            d_conv_bias_local,
            d_x_proj_local,
            d_dt_proj_local,
            d_bias_local,
            d_a_log,
            d_skip_local,
        ),
        "seq",
    )
    return (
        block_out,
        d_x_in,
        small_sums[0],
        d_w_in,
        small_sums[1],
        small_sums[2],
        small_sums[3],
        small_sums[4],
        small_sums[5],
        small_sums[6],
        small_sums[7],
        d_w_out,
    )


def solution(mesh):
    return jax.shard_map(
        shards,
        mesh=mesh,
        in_specs=(
            P("seq", None),
            P(),
            P(None, None, None, "ch"),
            P(None, "ch"),
            P("ch"),
            P("ch", None),
            P(None, "ch"),
            P("ch"),
            P(None, "ch"),
            P("ch"),
            P(None, None, "ch"),
            P(),
            P(),
            P("seq", "ch"),
        ),
        out_specs=(
            P("seq", "ch"),
            P("seq", "ch"),
            P("ch"),
            P(None, "seq", None, "ch"),
            P(None, "ch"),
            P("ch"),
            P("ch", None),
            P(None, "ch"),
            P("ch"),
            P(None, "ch"),
            P("ch"),
            P(None, "seq", "ch"),
        ),
        check_vma=False,
    )
```

time: 2870 us -> 672 us (0.23); the launches traced: 2820 us -> 663 us
  other arithmetic: 1710 us -> 25.2 us
  local copies, waits for them, and re-layouts: 492 us -> 67.5 us
  blocking collectives: 185 us -> 50.3 us
  waiting for transfers between devices: 285 us -> 375 us
    reduce_sum x289 -> x1, other arithmetic: 937 us -> 0.12 us  [doc_tables(): jnp.sum(jnp.where(order[:, None] >= order[None, :], doc_lengths[None, :],...]
    add x72 -> x0, other arithmetic: 548 us -> none  [the longest x32 333 us: run_span(): decay * state + (step_c[item] * conv_c[item])[None] * input_c[item][:, None]]
    mul x1280 -> x1, other arithmetic: 206 us -> 0.02 us  [shards(): rate_two = decay_rate * math.log2(math.e)]
    slice x163 -> x4, local copies, waits for them, and re-layouts: 171 us -> 4.63 us  [the longest x2 3.04 us: shards(): c_spread = mode_mask[:, :, None] * pair_cols[:, None, slab:]]
    mul x82 -> x0, local copies, waits for them, and re-layouts: 110 us -> none  [the longest x48 53.7 us: run_span(): (step_c[item] * conv_c[item])[None] * input_c[item][:, None]]
    all_gather x3 -> x0, blocking collectives: 106 us -> none  [carried_in_2(): gathered = jax.tree.map(lambda a: lax.all_gather(a, axis), part)]
    another operation x89 -> x4, local copies, waits for them, and re-layouts: 64.9 us -> 5.37 us  [own_columns(): return jnp.where(own, jnp.tile(values, (1, 16)), 0).astype(jnp.bfloat16)]
    all_gather x2 -> x4, waiting for transfers between devices: 153 us -> 204 us  [the longest x1 66.8 us: shards(): gated_all = lax.all_gather(gated, 'seq', axis=0, tiled=True)]
where the time goes in v1:
time: 672 us; the launch traced here: 663 us
  waiting for transfers between devices  375 us (56%)
  matrix products  92.7 us (14%)
  local copies, waits for them, and re-layouts  67.5 us (10%)
  blocking collectives  50.3 us (7%)
  other arithmetic  25.2 us (4%)
  Pallas kernels  24.8 us (4%)
  between operations  15.1 us (2%)
  starting transfers between devices  12.4 us (2%)
    psum x1, waiting for transfers between devices, shards(): lax.psum((d_gain_part, d_conv_weight_local, d_conv_bias_local, d_x_proj_l...  72.6 us
    all_gather x1, waiting for transfers between devices, shards(): gated_all = lax.all_gather(gated, 'seq', axis=0, tiled=True)  66.8 us
    all_gather x1, waiting for transfers between devices, shards(): d_x_all = lax.all_gather(d_x_branch, 'seq', axis=0, tiled=True)  66.8 us
    unnamed x155, local copies, waits for them, and re-layouts  49.5 us
    all_to_all x1, waiting for transfers between devices, shards(): lax.all_to_all(pair, 'seq', split_axis=1, concat_axis=0, tiled=True)  42.6 us
    psum x1, blocking collectives, shards(): lax.psum((d_gain_part, d_conv_weight_local, d_conv_bias_local, d_x_proj_l...  38.3 us
    all_gather x1, waiting for transfers between devices, shards(): d_z_all = lax.all_gather(d_z, 'seq', axis=0, tiled=True)  35.9 us
    all_gather x1, waiting for transfers between devices, shards(): lax.all_gather(scan_ends(masked_step, drive, d_ssm, b_wide, c_wide, rate_...  34.3 us
  transfers between devices with their start and end apart: 12, of which 10 were waited for; matrix products, arithmetic and copies ran while one was open for 11% of the time, Pallas kernels for 0%

profile of v1, /device:TPU:0, one launch (start us, length us, event | category | flops | bytes accessed | tf_op | source)
XLA Modules:
  0.0 662.9 jit_solution(15586020056217453386)
XLA Ops:
  13.4 25.7 %copy.115 = bf16[768,8,2,1024]{3,1,2,0:T(8,128)(2,1)} copy(bf16[768,8,2,1024]{3,2,1,0:T(2,128)(2,1)} %bitcast.250) | data formatting | bytes 50331648
  39.3 11.8 %convolution_convert_fusion = bf16[256,2048]{1,0:T(8,128)(2,1)S(1)} fusion(bf16[256,6144]{0,1:T(8,128)(2,1)S(1)} %bitcast.251, bf16[6144,2048]{1,0:T(8,128)(2,1)} %bitcast.249), kind=kOutput, calls=%fused_computation.18 | convolution fusion | flops 6442975232 | bytes 29360128 | tf_op jit(solution)/shard_map/dot_general | solution.py:226
  51.9 4.8 collective-permute-start
  59.5 15.3 %all-gather.7.cloned.1.call-done = bf16[256,2048]{0,1:T(8,128)(2,1)} async-done(((bf16[256,512]{0,1:T(8,128)(2,1)}), bf16[256,2048]{0,1:T(8,128)(2,1)}) %all-gather.7.cloned.1.call-update) | async-done | bytes 1048592 | tf_op jit(solution)/shard_map/all_gather | solution.py:263
  74.9 11.5 %multiply_reduce_fusion.3 = (f32[1024]{0:T(1024)}, f32[256,1024]{1,0:T(8,128)}, bf16[256,1024]{1,0:T(8,128)(2,1)S(1)}, f32[256,1024]{1,0:T(8,128)}, f32[256,1024]{1,0:T(8,128)}) fusion(bf16[256,1,1024]{2,0,1:T(8,128)(2,1)S(1)} %copy.114, f32[256]{0:T(256)S(1)} %get-tuple-element.139, f32[259,1024]{1,0:T(8,128)S(1)} %maximum_convert_fusion, ...), kind=kOutput, calls=%fused_computation.66 | convolution fusion | flops 3229613056 | bytes 22050304 | tf_op jit(solution)/shard_map/tmd,mde->te/dot_general | solution.py:265
  87.8 31.4 %all-reduce.7.cloned.1.call-done = f32[256,160]{0,1:T(8,128)} async-done(((f32[256,160]{0,1:T(8,128)}), f32[256,160]{0,1:T(8,128)}) %all-reduce.7.cloned.1.call-update) | async-done | bytes 163856 | tf_op jit(solution)/shard_map/psum | solution.py:248
  120.9 3.2 compare_select_fusion
  126.0 6.2 scan_ends.1
  142.9 34.3 %all-gather.15.cloned.1.call-done = f32[384,1024]{1,0:T(8,128)} async-done(((f32[48,1024]{1,0:T(8,128)}), f32[384,1024]{1,0:T(8,128)}) %all-gather.15.cloned.1.call-update) | async-done | bytes 1572880 | tf_op jit(solution)/shard_map/all_gather | solution.py:267
  180.8 4.5 scan_forward.1
  185.2 3.2 copy-done.2
  189.5 14.1 %scan_backward.1 = (f32[256,1024]{1,0:T(8,128)S(1)}, f32[256,1024]{1,0:T(8,128)S(1)}, f32[16,1,256]{2,1,0:T(1,128)S(1)}, f32[16,1,256]{2,1,0:T(1,128)S(1)}, f32[16,1024]{1,0:T(8,128)S(1)}) custom-call(f32[256,1024]{1,0:T(8,128)S(1)} %get-tuple-element.115.dtd_ref, f32[256,1024]{1,0:T(8,128)S(1)} %copy-done.9, f32[256,1024]{1,0:T(8,128)S(1)} %copy-done.8, ...), custom_call_target="tpu_custom_call" | custom-call | tf_op jit(solution)/shard_map/scan_backward/pallas_call | solution.py:170
  207.0 12.0 %all-reduce.12 = bf16[256,160]{0,1:T(8,128)(2,1)S(1)} all-reduce(f32[256,160]{0,1:T(8,128)S(1)} %pad_maximum_fusion.3), channel_id=1, replica_groups=mesh['seq'=8,'ch'=4] {'ch'}, use_global_device_ids=true, to_apply=%region_8.9 | all-reduce | flops 40960 | bytes 245760 | tf_op jit(solution)/shard_map/psum | solution.py:307
  219.1 4.3 multiply_reduce_fusion.7
  225.9 3.2 collective-permute-done.1
  229.9 24.1 %fusion.2 = f32[256,2048]{1,0:T(8,128)} fusion(bf16[3,2048,2,1024]{3,2,1,0:T(2,128)(2,1)} %param.16, f32[256,3]{0,1:T(4,128)S(1)} %copy-done.62, bf16[256,1,1024]{2,0,1:T(8,128)(2,1)S(1)} %bitcast.259, bf16[256,1,1024]{2,0,1:T(8,128)(2,1)S(1)} %bitcast.258), kind=kOutput, calls=%fused_computation.4 | convolution fusion | flops 6447169536 | bytes 28314624 | tf_op jit(solution)/shard_map/tk,mdk->tmd/dot_general | solution.py:341
  254.3 14.6 %multiply_reduce_fusion = f32[256,2048]{1,0:T(8,128)} fusion(bf16[3,2048,1024]{2,1,0:T(8,128)(2,1)} %param.24, f32[256,3]{0,1:T(4,128)S(1)} %copy-done.62, bf16[256,1024]{1,0:T(8,128)(2,1)S(1)} %get-tuple-element.110), kind=kOutput, calls=%fused_computation.5 | convolution fusion | flops 3223846912 | bytes 15207424 | tf_op jit(solution)/shard_map/te,mde->tmd/dot_general | solution.py:285
  271.0 2.8 pad_maximum_fusion.1
  273.8 5.1 all-to-all-start
  283.4 42.6 %all-to-all-done = bf16[256,8,512]{0,2,1:T(8,128)(2,1)} async-done(((bf16[256,8,512]{0,2,1:T(8,128)(2,1)}), bf16[256,8,512]{0,2,1:T(8,128)(2,1)}, u32[]{:S(2)}, u32[]{:S(2)}) %all-to-all-start) | async-done | bytes 2097184 | tf_op jit(solution)/shard_map/all_to_all | solution.py:359
  326.0 2.9 copy.106
  335.5 4.1 reduce-scatter.2.cloned.1.call-done
  339.5 2.4 multiply_reduce_fusion.8
  342.0 38.3 %all-reduce = (f32[512]{0:T(512)}, f32[4,1024]{1,0:T(4,128)}, f32[1024]{0:T(1024)}, f32[1024]{0:T(1024)}, f32[1024]{0:T(1024)}) all-reduce(f32[512]{0:T(512)S(1)} %get-tuple-element.107, f32[4,1024]{1,0:T(4,128)S(1)} %pad_maximum_fusion.4, f32[1024]{0:T(1024)S(1)} %get-tuple-element.90, ...), channel_id=1, replica_groups=mesh['seq'=8,'ch'=4] {'seq'}, use_global_device_ids=true, to_apply=%region_14.15 | all-reduce | flops 7680 | bytes 61440 | tf_op jit(solution)/shard_map/psum | solution.py:370
  380.3 35.9 %all-gather.11.cloned.1.call-done = bf16[2048,1024]{1,0:T(8,128)(2,1)} async-done(((bf16[256,1024]{1,0:T(8,128)(2,1)}), bf16[2048,1024]{1,0:T(8,128)(2,1)}) %all-gather.11.cloned.1.call-update) | async-done | bytes 4194320 | tf_op jit(solution)/shard_map/all_gather | solution.py:294
  416.1 7.3 %fusion.21 = f32[3,256,1,1024]{3,1,0,2:T(8,128)} fusion(bf16[2048,1024]{1,0:T(8,128)(2,1)} %all-gather.11.cloned.1.call-done, bf16[2048,256]{0,1:T(8,128)(2,1)S(1)} %copy.107, bf16[2048,3]{0,1:T(4,128)(2,1)S(1)} %fusion.104), kind=kOutput, calls=%fused_computation.24 | convolution fusion | flops 3222798336 | bytes 8400896 | tf_op jit(solution)/shard_map/tmd,te->mde/dot_general | solution.py:367
  423.4 66.8 %all-gather.13.cloned.1.call-done = bf16[2048,1024]{1,0:T(8,128)(2,1)} async-done(((bf16[256,1024]{1,0:T(8,128)(2,1)}), bf16[2048,1024]{1,0:T(8,128)(2,1)}) %all-gather.13.cloned.1.call-update) | async-done | bytes 4194320 | tf_op jit(solution)/shard_map/all_gather | solution.py:293
  490.2 7.3 %fusion.7 = f32[3,256,1024]{2,1,0:T(8,128)} fusion(bf16[2048,1024]{1,0:T(8,128)(2,1)} %all-gather.13.cloned.1.call-done, bf16[2048,256]{0,1:T(8,128)(2,1)S(1)} %copy.108, bf16[2048,3]{0,1:T(4,128)(2,1)S(1)} %fusion.104), kind=kOutput, calls=%fused_computation.10 | convolution fusion | flops 3222798336 | bytes 8400896 | tf_op jit(solution)/shard_map/tmd,te->mde/dot_general | solution.py:366
  497.4 66.8 %all-gather.9.cloned.1.call-done = bf16[2048,1024]{1,0:T(8,128)(2,1)} async-done(((bf16[256,1024]{1,0:T(8,128)(2,1)}), bf16[2048,1024]{1,0:T(8,128)(2,1)}) %all-gather.9.cloned.1.call-update) | async-done | bytes 4194320 | tf_op jit(solution)/shard_map/all_gather | solution.py:339
  564.2 5.3 fusion.16
  570.7 7.6 %copy.109 = f32[3,256,2,1024]{3,2,1,0:T(2,128)} copy(f32[3,256,2,1024]{3,1,0,2:T(8,128)S(1)} %pad_maximum_fusion) | data formatting | bytes 12582912
  578.3 72.6 %all-reduce.11.cloned.1.call-done = (f32[1024,160]{0,1:T(8,128)}, f32[128,1024]{1,0:T(8,128)}, f32[16,1024]{1,0:T(8,128)}) async-done(((f32[1024,160]{0,1:T(8,128)}, f32[128,1024]{1,0:T(8,128)}, f32[16,1024]{1,0:T(8,128)}), (f32[1024,160]{0,1:T(8,128)}, f32[128,1024]{1,0:T(8,128)}, f32[16,1024]{1,0:T(8,128)})) %all-reduce.11.cloned.1.call-update) | async-done | bytes 1245200 | tf_op jit(solution)/shard_map/psum | solution.py:370
  (234 shorter events, 56.0 us)
Async XLA Ops:
  7.2 79.3 %copy-start = (bf16[1024,160]{0,1:T(8,128)(2,1)S(1)}, bf16[1024,160]{0,1:T(8,128)(2,1)}, u32[]{:S(2)}) copy-start(bf16[1024,160]{0,1:T(8,128)(2,1)} %param.19) | copy-start | bytes 983044
  7.2 67.7 %all-gather.7.cloned.1.call-start = ((), (), s32[]{:S(2)}) async-start(), calls=%async_computation.3 | async-start | bytes 1310720 | tf_op jit(solution)/shard_map/all_gather | solution.py:263
  13.3 25.7 %copy-start.21 = (bf16[256,2048]{0,1:T(8,128)(2,1)}, bf16[256,2048]{0,1:T(8,128)(2,1)S(1)}, u32[]{:S(2)}) copy-start(bf16[256,2048]{0,1:T(8,128)(2,1)S(1)} %copy.91) | copy-start | bytes 3145732
  51.9 7.4 %collective-permute-start = (bf16[3,1024]{1,0:T(4,128)(2,1)S(1)}, bf16[3,1024]{1,0:T(4,128)(2,1)S(1)}, u32[]{:S(2)}, u32[]{:S(2)}) collective-permute-start(bf16[3,1024]{1,0:T(4,128)(2,1)S(1)} %bitcast.272), channel_id=1, source_target_pairs={{0,4},{4,8},{8,12},{12,16},{16,20},{20,24},{24,28},{1,5},{5,9},{9,... | collective-permute-start | bytes 18440 | tf_op jit(solution)/shard_map/ppermute | solution.py:17
  57.7 61.6 %all-reduce.7.cloned.1.call-start = ((), (), s32[]{:S(2)}) async-start(), calls=%async_computation.2 | async-start | bytes 327680 | tf_op jit(solution)/shard_map/psum | solution.py:248
  58.1 28.3 %copy-start.42 = (f32[1,1024]{1,0:T(1,128)}, f32[1,1024]{1,0:T(1,128)S(1)}, u32[]{:S(2)}) copy-start(f32[1,1024]{1,0:T(1,128)S(1)} %get-tuple-element.121) | copy-start | bytes 12292
  58.1 28.3 %copy-start.44 = (f32[1,1024]{1,0:T(1,128)}, f32[1,1024]{1,0:T(1,128)S(1)}, u32[]{:S(2)}) copy-start(f32[1,1024]{1,0:T(1,128)S(1)} %get-tuple-element.122) | copy-start | bytes 12292
  58.1 28.2 %copy-start.46 = (f32[1,1024]{1,0:T(1,128)}, f32[1,1024]{1,0:T(1,128)S(1)}, u32[]{:S(2)}) copy-start(f32[1,1024]{1,0:T(1,128)S(1)} %get-tuple-element.123) | copy-start | bytes 12292
  58.1 28.2 %copy-start.48 = (f32[1,1024]{1,0:T(1,128)}, f32[1,1024]{1,0:T(1,128)S(1)}, u32[]{:S(2)}) copy-start(f32[1,1024]{1,0:T(1,128)S(1)} %get-tuple-element.124) | copy-start | bytes 12292
  58.9 27.5 %copy-start.63 = (f32[256]{0:T(256)}, f32[256]{0:T(256)S(1)}, u32[]{:S(2)}) copy-start(f32[256]{0:T(256)S(1)} %get-tuple-element.137) | copy-start | bytes 3076
  58.9 27.5 %copy-start.65 = (f32[256]{0:T(256)}, f32[256]{0:T(256)S(1)}, u32[]{:S(2)}) copy-start(f32[256]{0:T(256)S(1)} %get-tuple-element.138) | copy-start | bytes 3076
  58.9 27.5 %copy-start.67 = (f32[256]{0:T(256)}, f32[256]{0:T(256)S(1)}, u32[]{:S(2)}) copy-start(f32[256]{0:T(256)S(1)} %get-tuple-element.139) | copy-start | bytes 3076
  58.9 27.5 %copy-start.69 = (f32[256]{0:T(256)}, f32[256]{0:T(256)S(1)}, u32[]{:S(2)}) copy-start(f32[256]{0:T(256)S(1)} %get-tuple-element.140) | copy-start | bytes 3076
  59.1 27.3 %copy-start.25 = (bf16[256,1,1024]{2,0,1:T(8,128)(2,1)}, bf16[256,1,1024]{2,0,1:T(8,128)(2,1)S(1)}, u32[]{:S(2)}) copy-start(bf16[256,1,1024]{2,0,1:T(8,128)(2,1)S(1)} %copy.114) | copy-start | bytes 1572868
  59.5 26.9 %copy-start.30 = (f32[259,1024]{1,0:T(8,128)}, f32[259,1024]{1,0:T(8,128)S(1)}, u32[]{:S(2)}) copy-start(f32[259,1024]{1,0:T(8,128)S(1)} %maximum_convert_fusion) | copy-start | bytes 3182596
  74.9 46.0 %copy-start.32 = (bf16[128,1024]{1,0:T(8,128)(2,1)S(1)}, bf16[128,1024]{1,0:T(8,128)(2,1)}, u32[]{:S(2)}) copy-start(bf16[128,1024]{1,0:T(8,128)(2,1)} %param.20) | copy-start | bytes 786436
  74.9 46.0 %copy-start.54 = (f32[1024]{0:T(1024)S(1)}, f32[1024]{0:T(1024)}, u32[]{:S(2)}) copy-start(f32[1024]{0:T(1024)} %param.21) | copy-start | bytes 12292
  86.4 37.7 %copy-start.19 = (bf16[256,1024]{1,0:T(8,128)(2,1)}, bf16[256,1024]{1,0:T(8,128)(2,1)S(1)}, u32[]{:S(2)}) copy-start(bf16[256,1024]{1,0:T(8,128)(2,1)S(1)} %get-tuple-element.103) | copy-start | bytes 1572868
  87.5 89.8 %all-gather.15.cloned.1.call-start = ((), (), s32[]{:S(2)}) async-start(), calls=%async_computation.9 | async-start | bytes 1769472 | tf_op jit(solution)/shard_map/all_gather | solution.py:267
  132.9 45.7 %copy-start.5 = (f32[256,16,128]{2,1,0:T(8,128)S(1)}, f32[256,16,128]{2,1,0:T(8,128)}, u32[]{:S(2)}) copy-start(f32[256,16,128]{2,1,0:T(8,128)} %copy-done.4) | copy-start | bytes 6291460
  132.9 200.5 %all-reduce.9.cloned.1.call-start = ((), (), s32[]{:S(2)}) async-start(), calls=%async_computation.5 | async-start | bytes 4194304 | tf_op jit(solution)/shard_map/psum | solution.py:349
  223.5 5.6 collective-permute-start.1
  225.9 28.1 %copy-start.29 = (bf16[256,1024]{1,0:T(8,128)(2,1)}, bf16[256,1024]{1,0:T(8,128)(2,1)S(1)}, u32[]{:S(2)}) copy-start(bf16[256,1024]{1,0:T(8,128)(2,1)S(1)} %get-tuple-element.109) | copy-start | bytes 1572868
  225.9 28.4 %copy-start.27 = (bf16[256,1024]{1,0:T(8,128)(2,1)}, bf16[256,1024]{1,0:T(8,128)(2,1)S(1)}, u32[]{:S(2)}) copy-start(bf16[256,1024]{1,0:T(8,128)(2,1)S(1)} %get-tuple-element.110) | copy-start | bytes 1572868
  229.8 24.2 %copy-start.28 = (bf16[256,1024]{1,0:T(8,128)(2,1)}, bf16[256,1024]{1,0:T(8,128)(2,1)S(1)}, u32[]{:S(2)}) copy-start(bf16[256,1024]{1,0:T(8,128)(2,1)S(1)} %fusion.45) | copy-start | bytes 1572868
  254.0 85.5 %reduce-scatter.2.cloned.1.call-start = ((), (), s32[]{:S(2)}) async-start(), calls=%async_computation.4 | async-start | bytes 2621440 | tf_op jit(solution)/shard_map/reduce_scatter | solution.py:287
  268.9 147.3 %all-gather.11.cloned.1.call-start = ((), (), s32[]{:S(2)}) async-start(), calls=%async_computation.7 | async-start | bytes 4718592 | tf_op jit(solution)/shard_map/all_gather | solution.py:294
  269.5 220.7 %all-gather.13.cloned.1.call-start = ((), (), s32[]{:S(2)}) async-start(), calls=%async_computation.8 | async-start | bytes 4718592 | tf_op jit(solution)/shard_map/all_gather | solution.py:293
  270.2 294.0 %all-gather.9.cloned.1.call-start = ((), (), s32[]{:S(2)}) async-start(), calls=%async_computation.6 | async-start | bytes 4718592 | tf_op jit(solution)/shard_map/all_gather | solution.py:339
  273.8 52.2 %all-to-all-start = ((bf16[256,8,512]{0,2,1:T(8,128)(2,1)}), bf16[256,8,512]{0,2,1:T(8,128)(2,1)}, u32[]{:S(2)}, u32[]{:S(2)}) async-start(bf16[256,8,512]{0,2,1:T(8,128)(2,1)} %pad_maximum_fusion.1), calls=%async_computation.1 | async-start | bytes 4194304 | tf_op jit(solution)/shard_map/all_to_all | solution.py:359
  278.8 372.0 %all-reduce.11.cloned.1.call-start = ((), (), s32[]{:S(2)}) async-start(), calls=%async_computation.10 | async-start | bytes 2490368 | tf_op jit(solution)/shard_map/psum | solution.py:370
  570.7 85.5 %copy-start.1 = (bf16[1024,160]{0,1:T(8,128)(2,1)S(1)}, bf16[1024,160]{0,1:T(8,128)(2,1)}, u32[]{:S(2)}) copy-start(bf16[1024,160]{0,1:T(8,128)(2,1)} %param.19) | copy-start | bytes 983044
  (53 other events, 358.3 us)
Sparse Core Ops, SparseCore 0:
  57.8 17.0 all-gather.6
  87.6 31.6 all-reduce.6
  133.0 44.1 all-gather.14
  254.2 51.4 all-reduce.8
  308.0 31.4 reduce-scatter.1
  342.3 73.8 all-gather.10
  418.5 71.6 all-gather.12
  492.5 71.6 all-gather.8
  569.7 81.1 all-reduce.10

commit v2 on v1

--- a/solution.py
+++ b/solution.py
@@ -15,6 +15,138 @@
     devices = range(lax.axis_size(axis))
     route = [(i - distance, i) for i in devices if i - distance in devices]
     return lax.ppermute(block, axis, route)
+
+
+MESH = pl.DeviceIdType.MESH
+
+
+def sum_over(part, axis):
+    count = lax.axis_size(axis)
+    sent = part.astype(jnp.bfloat16)
+    total = part
+    for distance in range(1, count):
+        route = [(i, (i + distance) % count) for i in range(count)]
+        total = total + lax.ppermute(sent, axis, route).astype(jnp.float32)
+    return total
+
+
+def sum_slices(part, axis):
+    count = lax.axis_size(axis)
+    place = lax.axis_index(axis)
+    width = part.shape[1] // count
+    total = lax.dynamic_slice_in_dim(part, place * width, width, 1)
+    sent = part.astype(jnp.bfloat16)
+    for distance in range(1, count):
+        route = [(i, (i + distance) % count) for i in range(count)]
+        piece = lax.dynamic_slice_in_dim(sent, (place + distance) % count * width, width, 1)
+        total = total + lax.ppermute(piece, axis, route).astype(jnp.float32)
+    return total
+
+
+def cycle_of(count):
+    across = count // 4
+    walk = [(0, x) for x in range(across)]
+    for turn, x in enumerate(reversed(range(across))):
+        column = [(z, x) for z in range(1, 4)]
+        walk += column[::-1] if turn % 2 else column
+    return [z * across + x for z, x in walk]
+
+
+def ring_gather(block, axis):
+    count = lax.axis_size(axis)
+    ring = cycle_of(count)
+    onward = [(ring[i], ring[(i + 1) % count]) for i in range(count)]
+    backward = [(b, a) for a, b in onward]
+    half = block.shape[0] // 2
+    ways = [[block[:half]], [block[half:]]]
+    for _ in range(count - 1):
+        ways[0].append(lax.ppermute(ways[0][-1], axis, onward))
+        ways[1].append(lax.ppermute(ways[1][-1], axis, backward))
+    return jnp.concatenate(ways[0] + ways[1], axis=0)
+
+
+def ring_exchange(pieces, axis):
+    count = lax.axis_size(axis)
+    place = lax.axis_index(axis)
+    ring = cycle_of(count)
+    where = {s: i for i, s in enumerate(ring)}
+    got = [lax.dynamic_index_in_dim(pieces, place, 1, False)]
+    for distance in range(1, count):
+        table = [ring[(where[s] + distance) % count] for s in range(count)]
+        piece = lax.dynamic_index_in_dim(pieces, jnp.array(table, jnp.int32)[place], 1, False)
+        got.append(lax.ppermute(piece, axis, list(enumerate(table))))
+    half = pieces.shape[0] // 2
+    first = [got[k][:half] for k in range(count)]
+    second = [got[-k][half:] for k in range(count)]
+    return jnp.concatenate(first + second, axis=0)
+
+
+def ring_modes(modes, axis):
+    count = lax.axis_size(axis)
+    place = lax.axis_index(axis)
+    ring = cycle_of(count)
+    where = {s: i for i, s in enumerate(ring)}
+    half = modes.shape[0] // (2 * count)
+    parts = []
+    for way in (0, 1):
+        for k in range(count):
+            step = k if way else -k
+            table = [ring[(where[s] + step) % count] for s in range(count)]
+            start = (2 * jnp.array(table, jnp.int32)[place] + way) * half
+            parts.append(lax.dynamic_slice_in_dim(modes, start, half))
+    return jnp.concatenate(parts)
+
+
+def states_kernel(count, ends_ref, steps_ref, ends_out, steps_out, send, recv):
+    me = lax.axis_index("seq")
+    barrier = pltpu.get_barrier_semaphore()
+    for distance in range(1, count):
+        peer = {"seq": lax.rem(me + distance, count)}
+        pl.semaphore_signal(barrier, inc=1, device_id=peer, device_id_type=MESH)
+    pl.semaphore_wait(barrier, count - 1)
+    copies = []
+    for distance in range(1, count):
+        peer = lax.rem(me + distance, count)
+        side = jnp.where(peer > me, 0, 1)
+        for kind, (source, target) in enumerate(
+            ((ends_ref.at[side], ends_out), (steps_ref, steps_out))
+        ):
+            copies.append(
+                pltpu.make_async_remote_copy(
+                    src_ref=source,
+                    dst_ref=target.at[distance - 1],
+                    send_sem=send.at[kind, distance - 1],
+                    recv_sem=recv.at[kind, distance - 1],
+                    device_id={"seq": peer},
+                    device_id_type=MESH,
+                )
+            )
+    for copy in copies:
+        copy.start()
+    for copy in copies:
+        copy.wait()
+
+
+def exchange_states(ends, steps):
+    others = lax.axis_size("seq") - 1
+    vmem = pl.BlockSpec(memory_space=pltpu.VMEM)
+    return pl.pallas_call(
+        functools.partial(states_kernel, others + 1),
+        in_specs=[vmem, vmem],
+        out_specs=[vmem, vmem],
+        out_shape=[
+            jax.ShapeDtypeStruct((others,) + ends.shape[1:], ends.dtype),
+            jax.ShapeDtypeStruct((others,) + steps.shape, steps.dtype),
+        ],
+        scratch_shapes=[
+            pltpu.SemaphoreType.DMA((2, others)),
+            pltpu.SemaphoreType.DMA((2, others)),
+        ],
+        compiler_params=pltpu.CompilerParams(
+            collective_id=0, has_side_effects=True, vmem_limit_bytes=32 << 20
+        ),
+        name="exchange_states",
+    )(ends, steps)
 
 
 def doc_tables(doc_lengths, positions):
@@ -40,28 +172,32 @@
 def tile_lanes(v, lanes):
     return jnp.concatenate([v] * (lanes // 128), axis=1)
 
-def ends_kernel(lb, dtd_ref, u_ref, g_ref, b_ref, c_ref, rate_ref, out_ref):
+def ends_kernel(lb, dtd_ref, u_ref, g_ref, b_ref, c_ref, rate_ref, out_ref, acc_ref):
     n = rate_ref.shape[0]
     rows, chans = dtd_ref.shape
     @pl.when(pl.program_id(0) == 0)
     def _():
-        out_ref[0:n, :] = jnp.zeros((n, chans), jnp.float32)
-        out_ref[n:2*n, :] = jnp.ones((n, chans), jnp.float32)
-        out_ref[2*n:3*n, :] = jnp.zeros((n, chans), jnp.float32)
+        acc_ref[0:n, :] = jnp.zeros((n, chans), jnp.float32)
+        acc_ref[n:2*n, :] = jnp.ones((n, chans), jnp.float32)
+        acc_ref[2*n:3*n, :] = jnp.zeros((n, chans), jnp.float32)
     for block in range(chans // lb):
         cut = slice(block * lb, (block + 1) * lb)
         rate = rate_ref[:, cut]
-        h = out_ref[0:n, cut]
-        reach = out_ref[n:2*n, cut]
-        head = out_ref[2*n:3*n, cut]
+        h = acc_ref[0:n, cut]
+        reach = acc_ref[n:2*n, cut]
+        head = acc_ref[2*n:3*n, cut]
         for t in range(rows):
             decay = jnp.exp2(dtd_ref[t:t+1, cut] * rate)
             h = decay * h + u_ref[t:t+1, cut] * tile_lanes(b_ref[t], lb)
             reach = reach * decay
             head = head + reach * (g_ref[t:t+1, cut] * tile_lanes(c_ref[t], lb))
-        out_ref[0:n, cut] = h
-        out_ref[n:2*n, cut] = reach
-        out_ref[2*n:3*n, cut] = head
+        acc_ref[0:n, cut] = h
+        acc_ref[n:2*n, cut] = reach
+        acc_ref[2*n:3*n, cut] = head
+    @pl.when(pl.program_id(0) == pl.num_programs(0) - 1)
+    def _():
+        out_ref[0] = acc_ref[0:n, :].astype(jnp.bfloat16)
+        out_ref[1] = acc_ref[2*n:3*n, :].astype(jnp.bfloat16)
 
 def scan_ends(dtd, u, g, b, c, rate, lb=LB, ch=CH):
     t, e = dtd.shape
@@ -72,8 +208,9 @@
         functools.partial(ends_kernel, lb),
         grid=(t // ch,),
         in_specs=[row, row, row, wide, wide, pl.BlockSpec((n, e), lambda i: (0, 0))],
-        out_specs=pl.BlockSpec((3 * n, e), lambda i: (0, 0)),
-        out_shape=jax.ShapeDtypeStruct((3 * n, e), jnp.float32),
+        out_specs=pl.BlockSpec((2, n, e), lambda i: (0, 0, 0)),
+        out_shape=jax.ShapeDtypeStruct((2, n, e), jnp.bfloat16),
+        scratch_shapes=[pltpu.VMEM((3 * n, e), jnp.float32)],
         compiler_params=pltpu.CompilerParams(vmem_limit_bytes=32 << 20),
         name="scan_ends",
     )(dtd, u, g, b, c, rate)
@@ -245,7 +382,7 @@
         )
     conv_out = jax.nn.silu(conv_pre).astype(jnp.bfloat16)
     conv_float = conv_out.astype(jnp.float32)
-    projected = lax.psum(jnp.dot(conv_out, x_proj, preferred_element_type=jnp.float32), "ch")
+    projected = sum_over(jnp.dot(conv_out, x_proj, preferred_element_type=jnp.float32), "ch")
     dt_low = projected[:, :rank_size].astype(jnp.bfloat16)
     b_in = projected[:, rank_size : rank_size + state_size]
     c_out = projected[:, rank_size + state_size :]
@@ -264,19 +401,28 @@
     cot_expanded = onehot[:, :, None] * cot_full[:, None, :]
     d_gated = jnp.einsum("tmd,mde->te", cot_expanded, w_out, preferred_element_type=jnp.float32)
     d_ssm = d_gated * gate_act
-    ends = lax.all_gather(
-        scan_ends(masked_step, drive, d_ssm, b_wide, c_wide, rate_two), "seq", axis=0
-    )
+    pair = jnp.concatenate(
+        [normed.reshape(tok_rows, seq_count, -1), cot_full.reshape(tok_rows, seq_count, -1)], axis=2
+    )
+    pair_cols = ring_exchange(pair, "seq")
+    masked_step, pair_cols = lax.optimization_barrier((masked_step, pair_cols))
+    ends = scan_ends(masked_step, drive, d_ssm, b_wide, c_wide, rate_two)
+    steps = jnp.sum(masked_step, axis=0)
+    ends_in, steps_in = exchange_states(ends, steps.reshape(8, -1))
+    steps_in = steps_in.reshape(seq_count - 1, inner_local)
     incoming = jnp.zeros((state_size, inner_local), jnp.float32)
     pending = incoming
-    for place in range(seq_count):
-        part = ends[place]
-        after = part[state_size : 2 * state_size] * incoming + part[:state_size]
-        incoming = jnp.where(place < seq_index, after, incoming)
-    for place in reversed(range(seq_count)):
-        part = ends[place]
-        after = part[state_size : 2 * state_size] * pending + part[2 * state_size :]
-        pending = jnp.where(place > seq_index, after, pending)
+    gap = jnp.zeros((inner_local,), jnp.float32)
+    for distance in range(1, seq_count):
+        part = ends_in[distance - 1].astype(jnp.float32) * jnp.exp2(rate_two * gap[None])
+        incoming = incoming + jnp.where(distance <= seq_index, part, 0.0)
+        gap = gap + steps_in[distance - 1]
+    gap = jnp.zeros((inner_local,), jnp.float32)
+    for distance in range(1, seq_count):
+        slot = seq_count - 1 - distance
+        part = ends_in[slot].astype(jnp.float32) * jnp.exp2(rate_two * gap[None])
+        pending = pending + jnp.where(distance + seq_index < seq_count, part, 0.0)
+        gap = gap + steps_in[slot]
     ssm, history = scan_forward(
         masked_step, drive, b_wide, own_columns(c_out), rate_two, incoming
     )
@@ -284,14 +430,14 @@
     gated = (ssm * gate_act).astype(jnp.bfloat16)
     proj_all = jnp.einsum("te,mde->tmd", gated, w_out, preferred_element_type=jnp.float32)
     mixer_part = jnp.sum(onehot.astype(jnp.float32)[:, :, None] * proj_all, axis=1)
-    mixer = lax.psum_scatter(mixer_part, "ch", scatter_dimension=1, tiled=True)
+    mixer = sum_slices(mixer_part, "ch")
     x_slice = lax.dynamic_slice_in_dim(x_full, ch_index * feat_part, feat_part, 1)
     block_out = (x_slice + mixer).astype(jnp.bfloat16)
     gate_sig = jax.nn.sigmoid(z_branch)
     d_z = d_gated * ssm * gate_sig * (1.0 + z_branch * (1.0 - gate_sig))
     d_z = d_z.astype(jnp.bfloat16)
-    gated_all = lax.all_gather(gated, "seq", axis=0, tiled=True)
-    d_z_all = lax.all_gather(d_z, "seq", axis=0, tiled=True)
+    gated_all = ring_gather(gated, "seq")
+    d_z_all = ring_gather(d_z, "seq")
     d_skip_local = jnp.sum(d_ssm * conv_float, axis=0)
     d_conv = d_ssm * d_skip[None]
     d_step, conv_grads, d_b, d_c, rate_grad = scan_backward(
@@ -304,7 +450,7 @@
     d_raw = d_full.astype(jnp.bfloat16)
     d_dt_proj_local = jnp.einsum("tr,te->re", dt_low, d_raw, preferred_element_type=jnp.float32)
     d_low_part = jnp.einsum("te,re->tr", d_raw, dt_proj, preferred_element_type=jnp.float32)
-    d_projected = lax.psum(jnp.concatenate([d_low_part, d_b, d_c], axis=1), "ch").astype(
+    d_projected = sum_over(jnp.concatenate([d_low_part, d_b, d_c], axis=1), "ch").astype(
         jnp.bfloat16
     )
     d_x_proj_local = jnp.einsum(
@@ -336,7 +482,7 @@
             d_x_branch + d_pre_ext[lag : lag + tok_rows] * conv_weight[offset][None] * same_doc
         )
     d_x_branch = d_x_branch.astype(jnp.bfloat16)
-    d_x_all = lax.all_gather(d_x_branch, "seq", axis=0, tiled=True)
+    d_x_all = ring_gather(d_x_branch, "seq")
     d_both = jnp.stack([d_x_branch, d_z], axis=1).reshape(tok_rows, 2 * inner_local)
     normed_terms = jnp.einsum(
         "tk,mdk->tmd",
@@ -346,19 +492,19 @@
     )
     normed_part = jnp.sum(onehot.astype(jnp.float32)[:, :, None] * normed_terms, axis=1)
     gain_slice = lax.dynamic_slice_in_dim(norm_gain, ch_index * feat_part, feat_part, 0)
-    d_normed = lax.psum(normed_part, "ch")
-    weighted = d_normed * norm_gain[None]
-    mean_term = jnp.mean(weighted * x_full, axis=1, keepdims=True)
-    d_slice = lax.dynamic_slice_in_dim(d_normed, ch_index * feat_part, feat_part, 1)
+    d_slice = sum_slices(normed_part, "ch")
+    own_dots = jnp.sum(normed_part * norm_gain[None] * x_full, axis=1)
+    dots = own_dots
+    for distance in range(1, ch_count):
+        route = [(i, (i + distance) % ch_count) for i in range(ch_count)]
+        dots = dots + lax.ppermute(own_dots, "ch", route)
+    mean_term = (dots / model_width)[:, None]
     weighted_slice = d_slice * gain_slice[None]
     d_x_in = cotangent.astype(jnp.float32) + scale * weighted_slice - x_slice * scale**3 * mean_term
     d_gain_part = jnp.sum(d_slice * x_slice * scale, axis=0)
-    pair = jnp.concatenate(
-        [normed.reshape(tok_rows, seq_count, -1), cot_full.reshape(tok_rows, seq_count, -1)], axis=2
-    ).reshape(tok_rows, -1)
-    pair_cols = lax.all_to_all(pair, "seq", split_axis=1, concat_axis=0, tiled=True)
+    all_modes = ring_modes(modes, "seq")
     slab = pair_cols.shape[1] // 2
-    mode_mask = (modes[:, None] == jnp.arange(mode_count, dtype=jnp.int32)[None]).astype(
+    mode_mask = (all_modes[:, None] == jnp.arange(mode_count, dtype=jnp.int32)[None]).astype(
         jnp.bfloat16
     )
     x_spread = mode_mask[:, :, None] * pair_cols[:, None, :slab]

time: 672 us -> 540 us (0.80)
  waiting for transfers between devices: 375 us -> 85.7 us
  local copies, waits for them, and re-layouts: 67.5 us -> 131 us
  starting transfers between devices: 12.4 us -> 72.4 us
  between operations: 15.1 us -> 37.9 us
  Pallas kernels: 24.8 us -> 38.9 us
  other arithmetic: 25.2 us -> 32.4 us
  blocking collectives: 50.3 us -> 43.3 us
    all_gather x4 -> x0, waiting for transfers between devices: 204 us -> none  [the longest x1 66.8 us: shards(): gated_all = lax.all_gather(gated, 'seq', axis=0, tiled=True)]
    ppermute x0 -> x64, waiting for transfers between devices: none -> 85.6 us  [the longest x21 36.9 us: ring_gather(): ways[0].append(lax.ppermute(ways[0][-1], axis, onward))]
    psum x1, waiting for transfers between devices: 72.6 us -> 0.01 us  [shards(): lax.psum((d_gain_part, d_conv_weight_local, d_conv_bias_local, d_x_proj_l...]
    ppermute x0 -> x64, starting transfers between devices: none -> 56.9 us  [the longest x21 19.4 us: ring_gather(): ways[0].append(lax.ppermute(ways[0][-1], axis, onward))]
    unnamed x155 -> x249, local copies, waits for them, and re-layouts: 49.5 us -> 102 us
    all_to_all x1 -> x0, waiting for transfers between devices: 42.6 us -> none  [shards(): lax.all_to_all(pair, 'seq', split_axis=1, concat_axis=0, tiled=True)]
    psum x2 -> x0, waiting for transfers between devices: 31.5 us -> none  [the longest x1 31.4 us: shards(): lax.psum(jnp.dot(conv_out, x_proj, preferred_element_type=jnp.float32), '...]
    all_gather x1, waiting for transfers between devices: 15.3 us -> 0.01 us  [shards(): cot_full = lax.all_gather(cotangent, 'ch', axis=1, tiled=True)]
  transfers between devices with their start and end apart: 12 -> 68, of which waited for: 10 -> 24; matrix products, arithmetic and copies ran while one was open for 11% -> 30% of each run, Pallas kernels for 0% -> 0%
where the time goes in v2:
time: 540 us; the launch traced here: 529 us
  local copies, waits for them, and re-layouts  131 us (24%)
  matrix products  87.2 us (16%)
  waiting for transfers between devices  85.7 us (16%)
  starting transfers between devices  72.4 us (13%)
  blocking collectives  43.3 us (8%)
  Pallas kernels  38.9 us (7%)
  between operations  37.9 us (7%)
  other arithmetic  32.4 us (6%)
    unnamed x249, local copies, waits for them, and re-layouts  102 us
    psum x1, blocking collectives, shards(): lax.psum((d_gain_part, d_conv_weight_local, d_conv_bias_local, d_x_proj_l...  43.3 us
    ppermute x21, waiting for transfers between devices, ring_gather(): ways[0].append(lax.ppermute(ways[0][-1], axis, onward))  36.9 us
    ppermute x21, waiting for transfers between devices, ring_gather(): ways[1].append(lax.ppermute(ways[1][-1], axis, backward))  26.1 us
    dot_general x1, matrix products, shards(): jnp.einsum('tk,mdk->tmd', d_both, w_in.reshape(mode_count, model_width, 2...  24.3 us
    ppermute x7, waiting for transfers between devices, ring_exchange(): got.append(lax.ppermute(piece, axis, list(enumerate(table))))  21.2 us
    ppermute x21, starting transfers between devices, ring_gather(): ways[0].append(lax.ppermute(ways[0][-1], axis, onward))  19.4 us
    ppermute x21, starting transfers between devices, ring_gather(): ways[1].append(lax.ppermute(ways[1][-1], axis, backward))  19.2 us
  transfers between devices with their start and end apart: 68, of which 24 were waited for; matrix products, arithmetic and copies ran while one was open for 30% of the time, Pallas kernels for 0%

profile of v2, /device:TPU:0, one launch (start us, length us, event | category | flops | bytes accessed | tf_op | source)
XLA Modules:
  0.0 529.2 jit_solution(13746171416526763903)
XLA Ops:
  12.8 25.3 %copy.188 = bf16[768,8,2,1024]{3,1,2,0:T(8,128)(2,1)} copy(bf16[768,8,2,1024]{3,2,1,0:T(2,128)(2,1)} %bitcast.221) | data formatting | bytes 50331648
  38.4 12.8 %convolution_convert_fusion = bf16[256,2048]{1,0:T(8,128)(2,1)} fusion(bf16[256,6144]{0,1:T(8,128)(2,1)S(1)} %bitcast.224, bf16[6144,2048]{1,0:T(8,128)(2,1)} %bitcast.220), kind=kOutput, calls=%fused_computation.34 | convolution fusion | flops 6442975232 | bytes 29360128 | tf_op jit(solution)/shard_map/dot_general | solution.py:363
  55.3 5.4 %collective-permute-start = (bf16[3,1024]{1,0:T(4,128)(2,1)}, bf16[3,1024]{1,0:T(4,128)(2,1)}, u32[]{:S(2)}, u32[]{:S(2)}) collective-permute-start(bf16[3,1024]{1,0:T(4,128)(2,1)} %bitcast.3), channel_id=1, source_target_pairs={{0,4},{4,8},{8,12},{12,16},{16,20},{20,24},{24,28},{1,5},{5,9},{9,... | collective-permute-start | bytes 18440 | tf_op jit(solution)/shard_map/ppermute | solution.py:17
  102.1 12.5 %multiply_reduce_fusion.3 = (f32[1024]{0:T(1024)}, f32[256,1024]{1,0:T(8,128)S(1)}, bf16[256,1024]{1,0:T(8,128)(2,1)S(1)}, f32[256,1024]{1,0:T(8,128)}, f32[256,1024]{1,0:T(8,128)}) fusion(bf16[256,1,1024]{2,0,1:T(8,128)(2,1)S(1)} %copy.187, f32[256]{0:T(256)} %get-tuple-element.190, f32[259,1024]{1,0:T(8,128)} %maximum_convert_fusion, ...), kind=kOutput, calls=%fused_computation.81 | convolution fusion | flops 3229613056 | bytes 22050304 | tf_op jit(solution)/shard_map/tmd,mde->te/dot_general | solution.py:402
  142.6 15.3 %collective-permute-done.5 = bf16[256,512]{0,1:T(8,128)(2,1)} collective-permute-done((bf16[256,512]{0,1:T(8,128)(2,1)}, bf16[256,512]{0,1:T(8,128)(2,1)}, u32[]{:S(2)}, u32[]{:S(2)}) %collective-permute-start.5) | collective-permute-done | bytes 262176 | tf_op jit(solution)/shard_map/ppermute | solution.py:77
  162.6 3.4 collective-permute-done.8
  185.5 6.2 %scan_ends.1.ends_ref = bf16[2,16,1024]{2,1,0:T(8,128)(2,1)S(1)} custom-call(f32[256,1024]{1,0:T(8,128)S(1)} %get-tuple-element.23.dtd_ref, f32[256,1024]{1,0:T(8,128)S(1)} %get-tuple-element.141.u_ref, f32[256,1024]{1,0:T(8,128)S(1)} %get-tuple-element.110.g_ref, f32[256,16,128]{2,1,0:T(8,128)S(1)} %broadcast_in_dim.59.b_ref, ...), custom_call_target="tpu_custom_call" | custom-call | tf_op jit(solution)/shard_map/scan_ends/pallas_call | solution.py:207
  191.8 14.1 %exchange_states.1 = (bf16[7,16,1024]{2,1,0:T(8,128)(2,1)S(1)}, f32[7,8,128]{2,1,0:T(8,128)S(1)}) custom-call(bf16[2,16,1024]{2,1,0:T(8,128)(2,1)S(1)} %scan_ends.1.ends_ref, f32[8,128]{1,0:T(8,128)S(1)} %bitcast.219), custom_call_target="tpu_custom_call" | custom-call | tf_op jit(solution)/shard_map/exchange_states/pallas_call | solution.py:133
  206.1 4.5 scan_forward.1
  210.5 3.3 copy-done.2
  214.1 14.1 %scan_backward.1 = (f32[256,1024]{1,0:T(8,128)S(1)}, f32[256,1024]{1,0:T(8,128)S(1)}, f32[16,1,256]{2,1,0:T(1,128)S(1)}, f32[16,1,256]{2,1,0:T(1,128)S(1)}, f32[16,1024]{1,0:T(8,128)S(1)}) custom-call(f32[256,1024]{1,0:T(8,128)S(1)} %get-tuple-element.23.dtd_ref, f32[256,1024]{1,0:T(8,128)S(1)} %copy-done.7, f32[256,1024]{1,0:T(8,128)S(1)} %copy-done.6, ...), custom_call_target="tpu_custom_call" | custom-call | tf_op jit(solution)/shard_map/scan_backward/pallas_call | solution.py:307
  240.8 13.3 %multiply_reduce_fusion = f32[256,2048]{1,0:T(8,128)S(1)} fusion(bf16[3,2048,1024]{2,1,0:T(8,128)(2,1)} %param.47, f32[256,3]{0,1:T(4,128)S(1)} %copy-done.64, bf16[256,1024]{1,0:T(8,128)(2,1)S(1)} %get-tuple-element.122), kind=kOutput, calls=%fused_computation.5 | convolution fusion | flops 3223846912 | bytes 15207424 | tf_op jit(solution)/shard_map/te,mde->tmd/dot_general | solution.py:431
  263.7 10.0 %collective-permute-start.17 = (f32[3,1024]{1,0:T(4,128)S(1)}, f32[3,1024]{1,0:T(4,128)S(1)}, u32[]{:S(2)}, u32[]{:S(2)}) collective-permute-start(f32[3,1024]{1,0:T(4,128)S(1)} %slice.323), channel_id=1, source_target_pairs={{4,0},{8,4},{12,8},{16,12},{20,16},{24,20},{28,24},{5,1},{9,5},{13... | collective-permute-start | bytes 36872 | tf_op jit(solution)/shard_map/ppermute | solution.py:17
  275.2 24.3 %fusion.2 = f32[256,2048]{1,0:T(8,128)} fusion(bf16[3,2048,2,1024]{3,2,1,0:T(2,128)(2,1)} %param.39, f32[256,3]{0,1:T(4,128)S(1)} %copy-done.64, bf16[256,1,1024]{2,0,1:T(8,128)(2,1)S(1)} %bitcast.229, bf16[256,1,1024]{2,0,1:T(8,128)(2,1)S(1)} %bitcast.230), kind=kOutput, calls=%fused_computation.4 | convolution fusion | flops 6447169536 | bytes 28314624 | tf_op jit(solution)/shard_map/tk,mdk->tmd/dot_general | solution.py:487
  299.5 3.7 fusion.122
  309.7 2.6 collective-permute-start.38
  316.6 13.9 %collective-permute-done.38 = bf16[128,1024]{1,0:T(8,128)(2,1)S(1)} collective-permute-done((bf16[128,1024]{1,0:T(8,128)(2,1)}, bf16[128,1024]{1,0:T(8,128)(2,1)S(1)}, u32[]{:S(2)}, u32[]{:S(2)}) %collective-permute-start.38) | collective-permute-done | bytes 262176 | tf_op jit(solution)/shard_map/ppermute | solution.py:63
  331.4 7.9 %collective-permute-done.52 = bf16[128,1024]{1,0:T(8,128)(2,1)S(1)} collective-permute-done((bf16[128,1024]{1,0:T(8,128)(2,1)}, bf16[128,1024]{1,0:T(8,128)(2,1)S(1)}, u32[]{:S(2)}, u32[]{:S(2)}) %collective-permute-start.52) | collective-permute-done | bytes 262176 | tf_op jit(solution)/shard_map/ppermute | solution.py:63
  344.9 4.9 collective-permute-done.24
  352.1 5.4 %collective-permute-done.39 = bf16[128,1024]{1,0:T(8,128)(2,1)} collective-permute-done((bf16[128,1024]{1,0:T(8,128)(2,1)S(1)}, bf16[128,1024]{1,0:T(8,128)(2,1)}, u32[]{:S(2)}, u32[]{:S(2)}) %collective-permute-start.39) | collective-permute-done | bytes 262176 | tf_op jit(solution)/shard_map/ppermute | solution.py:63
  358.7 2.9 multiply_reduce_fusion.8
  367.2 43.3 %all-reduce = (f32[512]{0:T(512)}, f32[4,1024]{1,0:T(4,128)}, f32[1024]{0:T(1024)}, f32[1024]{0:T(1024)}, f32[1024]{0:T(1024)}) all-reduce(f32[512]{0:T(512)S(1)} %get-tuple-element.119, f32[4,1024]{1,0:T(4,128)S(1)} %pad_maximum_fusion.3, f32[1024]{0:T(1024)S(1)} %get-tuple-element.98, ...), channel_id=1, replica_groups=mesh['seq'=8,'ch'=4] {'seq'}, use_global_device_ids=true, to_apply=%region_11.12 | all-reduce | flops 7680 | bytes 61440 | tf_op jit(solution)/shard_map/psum | solution.py:516
  427.5 3.6 collective-permute-done.48
  433.8 2.9 collective-permute-done.62
  445.0 2.9 collective-permute-done.49
  453.6 5.5 %collective-permute-done.35 = bf16[128,1024]{1,0:T(8,128)(2,1)S(1)} collective-permute-done((bf16[128,1024]{1,0:T(8,128)(2,1)S(1)}, bf16[128,1024]{1,0:T(8,128)(2,1)S(1)}, u32[]{:S(2)}, u32[]{:S(2)}) %collective-permute-start.35) | collective-permute-done | bytes 262176 | tf_op jit(solution)/shard_map/ppermute | solution.py:64
  461.9 3.0 collective-permute-done.57
  471.2 4.8 collective-permute-done.36
  485.5 5.3 fusion.21
  491.0 5.1 fusion.7
  502.7 5.2 fusion.16
  509.0 7.6 %copy.174 = f32[3,256,2,1024]{3,2,1,0:T(2,128)} copy(f32[3,256,2,1024]{3,1,0,2:T(8,128)S(1)} %pad_maximum_fusion) | data formatting | bytes 12582912
  (456 shorter events, 196.3 us)
Async XLA Ops:
  7.2 94.9 %all-gather.2.cloned.1.call-start = ((), (), s32[]{:S(2)}) async-start(), calls=%async_computation | async-start | bytes 1310720 | tf_op jit(solution)/shard_map/all_gather | solution.py:400
  55.3 45.0 %collective-permute-start = (bf16[3,1024]{1,0:T(4,128)(2,1)}, bf16[3,1024]{1,0:T(4,128)(2,1)}, u32[]{:S(2)}, u32[]{:S(2)}) collective-permute-start(bf16[3,1024]{1,0:T(4,128)(2,1)} %bitcast.3), channel_id=1, source_target_pairs={{0,4},{4,8},{8,12},{12,16},{16,20},{20,24},{24,28},{1,5},{5,9},{9,... | collective-permute-start | bytes 18440 | tf_op jit(solution)/shard_map/ppermute | solution.py:17
  62.5 454.1 %all-reduce.4.cloned.1.call-start = ((), (), s32[]{:S(2)}) async-start(), calls=%async_computation.1 | async-start | bytes 2490368 | tf_op jit(solution)/shard_map/psum | solution.py:516
  119.9 21.1 %collective-permute-start.4 = (bf16[256,512]{0,1:T(8,128)(2,1)}, bf16[256,512]{0,1:T(8,128)(2,1)}, u32[]{:S(2)}, u32[]{:S(2)}) collective-permute-start(bf16[256,512]{0,1:T(8,128)(2,1)} %get-tuple-element.130), channel_id=1, source_target_pairs={{0,4},{4,12},{8,0},{12,20},{16,8},{20,28},{24,16},{28,24},{1,5},{5... | collective-permute-start | bytes 786440 | tf_op jit(solution)/shard_map/ppermute | solution.py:77
  120.9 37.0 %collective-permute-start.5 = (bf16[256,512]{0,1:T(8,128)(2,1)}, bf16[256,512]{0,1:T(8,128)(2,1)}, u32[]{:S(2)}, u32[]{:S(2)}) collective-permute-start(bf16[256,512]{0,1:T(8,128)(2,1)} %get-tuple-element.131), channel_id=1, source_target_pairs={{0,12},{4,20},{8,4},{12,28},{16,0},{20,24},{24,8},{28,16},{1,13},{... | collective-permute-start | bytes 786440 | tf_op jit(solution)/shard_map/ppermute | solution.py:77
  124.3 35.1 %collective-permute-start.6 = (bf16[256,512]{0,1:T(8,128)(2,1)}, bf16[256,512]{0,1:T(8,128)(2,1)}, u32[]{:S(2)}, u32[]{:S(2)}) collective-permute-start(bf16[256,512]{0,1:T(8,128)(2,1)} %get-tuple-element.132), channel_id=1, source_target_pairs={{0,20},{4,28},{8,12},{12,24},{16,4},{20,16},{24,0},{28,8},{1,21},{... | collective-permute-start | bytes 786440 | tf_op jit(solution)/shard_map/ppermute | solution.py:77
  125.7 35.4 %collective-permute-start.7 = (bf16[256,512]{0,1:T(8,128)(2,1)}, bf16[256,512]{0,1:T(8,128)(2,1)}, u32[]{:S(2)}, u32[]{:S(2)}) collective-permute-start(bf16[256,512]{0,1:T(8,128)(2,1)} %get-tuple-element.133), channel_id=1, source_target_pairs={{0,28},{4,24},{8,20},{12,16},{16,12},{20,8},{24,4},{28,0},{1,29},{... | collective-permute-start | bytes 786440 | tf_op jit(solution)/shard_map/ppermute | solution.py:77
  128.1 38.0 %collective-permute-start.8 = (bf16[256,512]{0,1:T(8,128)(2,1)}, bf16[256,512]{0,1:T(8,128)(2,1)}, u32[]{:S(2)}, u32[]{:S(2)}) collective-permute-start(bf16[256,512]{0,1:T(8,128)(2,1)} %get-tuple-element.135), channel_id=1, source_target_pairs={{0,24},{4,16},{8,28},{12,8},{16,20},{20,0},{24,12},{28,4},{1,25},{... | collective-permute-start | bytes 786440 | tf_op jit(solution)/shard_map/ppermute | solution.py:77
  141.0 26.6 %collective-permute-start.9 = (bf16[256,512]{0,1:T(8,128)(2,1)}, bf16[256,512]{0,1:T(8,128)(2,1)S(1)}, u32[]{:S(2)}, u32[]{:S(2)}) collective-permute-start(bf16[256,512]{0,1:T(8,128)(2,1)} %get-tuple-element.134), channel_id=1, source_target_pairs={{0,16},{4,8},{8,24},{12,0},{16,28},{20,4},{24,20},{28,12},{1,17},{... | collective-permute-start | bytes 786440 | tf_op jit(solution)/shard_map/ppermute | solution.py:77
  235.2 25.3 %collective-permute-start.16 = (bf16[256,160]{0,1:T(8,128)(2,1)}, bf16[256,160]{0,1:T(8,128)(2,1)}, u32[]{:S(2)}, u32[]{:S(2)}) collective-permute-start(bf16[256,160]{0,1:T(8,128)(2,1)} %fusion.82), channel_id=1, source_target_pairs={{0,3},{1,0},{2,1},{3,2},{4,7},{5,4},{6,5},{7,6},{8,11},{9,8},{10,9... | collective-permute-start | bytes 245768 | tf_op jit(solution)/shard_map/ppermute | solution.py:29
  235.2 25.3 %collective-permute-start.15 = (bf16[256,160]{0,1:T(8,128)(2,1)}, bf16[256,160]{0,1:T(8,128)(2,1)}, u32[]{:S(2)}, u32[]{:S(2)}) collective-permute-start(bf16[256,160]{0,1:T(8,128)(2,1)} %fusion.82), channel_id=1, source_target_pairs={{0,2},{1,3},{2,0},{3,1},{4,6},{5,7},{6,4},{7,5},{8,10},{9,11},{10,... | collective-permute-start | bytes 245768 | tf_op jit(solution)/shard_map/ppermute | solution.py:29
  236.0 24.5 %collective-permute-start.14 = (bf16[256,160]{0,1:T(8,128)(2,1)}, bf16[256,160]{0,1:T(8,128)(2,1)}, u32[]{:S(2)}, u32[]{:S(2)}) collective-permute-start(bf16[256,160]{0,1:T(8,128)(2,1)} %fusion.82), channel_id=1, source_target_pairs={{0,1},{1,2},{2,3},{3,0},{4,5},{5,6},{6,7},{7,4},{8,9},{9,10},{10,1... | collective-permute-start | bytes 245768 | tf_op jit(solution)/shard_map/ppermute | solution.py:29
  255.3 58.4 %collective-permute-start.13 = (bf16[256,512]{1,0:T(8,128)(2,1)}, bf16[256,512]{1,0:T(8,128)(2,1)}, u32[]{:S(2)}, u32[]{:S(2)}) collective-permute-start(bf16[256,512]{1,0:T(8,128)(2,1)} %get-tuple-element.143), channel_id=1, source_target_pairs={{0,3},{1,0},{2,1},{3,2},{4,7},{5,4},{6,5},{7,6},{8,11},{9,8},{10,9... | collective-permute-start | bytes 786440 | tf_op jit(solution)/shard_map/ppermute | solution.py:42
  256.9 57.5 %collective-permute-start.12 = (bf16[256,512]{1,0:T(8,128)(2,1)}, bf16[256,512]{1,0:T(8,128)(2,1)}, u32[]{:S(2)}, u32[]{:S(2)}) collective-permute-start(bf16[256,512]{1,0:T(8,128)(2,1)} %get-tuple-element.144), channel_id=1, source_target_pairs={{0,2},{1,3},{2,0},{3,1},{4,6},{5,7},{6,4},{7,5},{8,10},{9,11},{10,... | collective-permute-start | bytes 786440 | tf_op jit(solution)/shard_map/ppermute | solution.py:42
  260.5 55.2 %collective-permute-start.11 = (bf16[256,512]{1,0:T(8,128)(2,1)}, bf16[256,512]{1,0:T(8,128)(2,1)}, u32[]{:S(2)}, u32[]{:S(2)}) collective-permute-start(bf16[256,512]{1,0:T(8,128)(2,1)} %get-tuple-element.142), channel_id=1, source_target_pairs={{0,1},{1,2},{2,3},{3,0},{4,5},{5,6},{6,7},{7,4},{8,9},{9,10},{10,1... | collective-permute-start | bytes 786440 | tf_op jit(solution)/shard_map/ppermute | solution.py:42
  309.7 20.8 %collective-permute-start.38 = (bf16[128,1024]{1,0:T(8,128)(2,1)}, bf16[128,1024]{1,0:T(8,128)(2,1)S(1)}, u32[]{:S(2)}, u32[]{:S(2)}) collective-permute-start(bf16[128,1024]{1,0:T(8,128)(2,1)} %get-tuple-element.155), channel_id=1, source_target_pairs={{0,4},{4,12},{12,20},{20,28},{28,24},{24,16},{16,8},{8,0},{1,5},{5... | collective-permute-start | bytes 786440 | tf_op jit(solution)/shard_map/ppermute | solution.py:63
  312.3 19.1 %collective-permute-start.45 = (bf16[128,1024]{1,0:T(8,128)(2,1)}, bf16[128,1024]{1,0:T(8,128)(2,1)S(1)}, u32[]{:S(2)}, u32[]{:S(2)}) collective-permute-start(bf16[128,1024]{1,0:T(8,128)(2,1)} %get-tuple-element.153), channel_id=1, source_target_pairs={{4,0},{12,4},{20,12},{28,20},{24,28},{16,24},{8,16},{0,8},{5,1},{1... | collective-permute-start | bytes 786440 | tf_op jit(solution)/shard_map/ppermute | solution.py:64
  313.7 25.6 %collective-permute-start.52 = (bf16[128,1024]{1,0:T(8,128)(2,1)}, bf16[128,1024]{1,0:T(8,128)(2,1)S(1)}, u32[]{:S(2)}, u32[]{:S(2)}) collective-permute-start(bf16[128,1024]{1,0:T(8,128)(2,1)} %get-tuple-element.149), channel_id=1, source_target_pairs={{0,4},{4,12},{12,20},{20,28},{28,24},{24,16},{16,8},{8,0},{1,5},{5... | collective-permute-start | bytes 786440 | tf_op jit(solution)/shard_map/ppermute | solution.py:63
  314.3 25.0 %collective-permute-start.59 = (bf16[128,1024]{1,0:T(8,128)(2,1)}, bf16[128,1024]{1,0:T(8,128)(2,1)S(1)}, u32[]{:S(2)}, u32[]{:S(2)}) collective-permute-start(bf16[128,1024]{1,0:T(8,128)(2,1)} %get-tuple-element.147), channel_id=1, source_target_pairs={{4,0},{12,4},{20,12},{28,20},{24,28},{16,24},{8,16},{0,8},{5,1},{1... | collective-permute-start | bytes 786440 | tf_op jit(solution)/shard_map/ppermute | solution.py:64
  315.7 25.6 %collective-permute-start.20 = (bf16[256,512]{1,0:T(8,128)(2,1)S(1)}, bf16[256,512]{1,0:T(8,128)(2,1)S(1)}, u32[]{:S(2)}, u32[]{:S(2)}) collective-permute-start(bf16[256,512]{1,0:T(8,128)(2,1)S(1)} %get-tuple-element.137), channel_id=1, source_target_pairs={{0,3},{1,0},{2,1},{3,2},{4,7},{5,4},{6,5},{7,6},{8,11},{9,8},{10,9... | collective-permute-start | bytes 786440 | tf_op jit(solution)/shard_map/ppermute | solution.py:42
  342.8 20.7 %collective-permute-start.53 = (bf16[128,1024]{1,0:T(8,128)(2,1)S(1)}, bf16[128,1024]{1,0:T(8,128)(2,1)}, u32[]{:S(2)}, u32[]{:S(2)}) collective-permute-start(bf16[128,1024]{1,0:T(8,128)(2,1)S(1)} %collective-permute-done.52), channel_id=1, source_target_pairs={{0,4},{4,12},{12,20},{20,28},{28,24},{24,16},{16,8},{8,0},{1,5},{5... | collective-permute-start | bytes 786440 | tf_op jit(solution)/shard_map/ppermute | solution.py:63
  344.3 17.3 %collective-permute-start.46 = (bf16[128,1024]{1,0:T(8,128)(2,1)S(1)}, bf16[128,1024]{1,0:T(8,128)(2,1)S(1)}, u32[]{:S(2)}, u32[]{:S(2)}) collective-permute-start(bf16[128,1024]{1,0:T(8,128)(2,1)S(1)} %collective-permute-done.45), channel_id=1, source_target_pairs={{4,0},{12,4},{20,12},{28,20},{24,28},{16,24},{8,16},{0,8},{5,1},{1... | collective-permute-start | bytes 786440 | tf_op jit(solution)/shard_map/ppermute | solution.py:64
  350.9 59.7 %collective-permute-start.25 = (bf16[128,1024]{1,0:T(8,128)(2,1)}, bf16[128,1024]{1,0:T(8,128)(2,1)}, u32[]{:S(2)}, u32[]{:S(2)}) collective-permute-start(bf16[128,1024]{1,0:T(8,128)(2,1)} %collective-permute-done.24), channel_id=1, source_target_pairs={{0,4},{4,12},{12,20},{20,28},{28,24},{24,16},{16,8},{8,0},{1,5},{5... | collective-permute-start | bytes 786440 | tf_op jit(solution)/shard_map/ppermute | solution.py:63
  357.5 53.0 %collective-permute-start.32 = (bf16[128,1024]{1,0:T(8,128)(2,1)S(1)}, bf16[128,1024]{1,0:T(8,128)(2,1)S(1)}, u32[]{:S(2)}, u32[]{:S(2)}) collective-permute-start(bf16[128,1024]{1,0:T(8,128)(2,1)S(1)} %collective-permute-done.31), channel_id=1, source_target_pairs={{4,0},{12,4},{20,12},{28,20},{24,28},{16,24},{8,16},{0,8},{5,1},{1... | collective-permute-start | bytes 786440 | tf_op jit(solution)/shard_map/ppermute | solution.py:64
  361.5 54.4 %collective-permute-start.40 = (bf16[128,1024]{1,0:T(8,128)(2,1)}, bf16[128,1024]{1,0:T(8,128)(2,1)}, u32[]{:S(2)}, u32[]{:S(2)}) collective-permute-start(bf16[128,1024]{1,0:T(8,128)(2,1)} %collective-permute-done.39), channel_id=1, source_target_pairs={{0,4},{4,12},{12,20},{20,28},{28,24},{24,16},{16,8},{8,0},{1,5},{5... | collective-permute-start | bytes 786440 | tf_op jit(solution)/shard_map/ppermute | solution.py:63
  363.5 52.4 %collective-permute-start.47 = (bf16[128,1024]{1,0:T(8,128)(2,1)S(1)}, bf16[128,1024]{1,0:T(8,128)(2,1)}, u32[]{:S(2)}, u32[]{:S(2)}) collective-permute-start(bf16[128,1024]{1,0:T(8,128)(2,1)S(1)} %collective-permute-done.46), channel_id=1, source_target_pairs={{4,0},{12,4},{20,12},{28,20},{24,28},{16,24},{8,16},{0,8},{5,1},{1... | collective-permute-start | bytes 786440 | tf_op jit(solution)/shard_map/ppermute | solution.py:64
  364.5 53.5 %collective-permute-start.54 = (bf16[128,1024]{1,0:T(8,128)(2,1)}, bf16[128,1024]{1,0:T(8,128)(2,1)}, u32[]{:S(2)}, u32[]{:S(2)}) collective-permute-start(bf16[128,1024]{1,0:T(8,128)(2,1)} %collective-permute-done.53), channel_id=1, source_target_pairs={{0,4},{4,12},{12,20},{20,28},{28,24},{24,16},{16,8},{8,0},{1,5},{5... | collective-permute-start | bytes 786440 | tf_op jit(solution)/shard_map/ppermute | solution.py:63
  442.4 16.7 %collective-permute-start.35 = (bf16[128,1024]{1,0:T(8,128)(2,1)S(1)}, bf16[128,1024]{1,0:T(8,128)(2,1)S(1)}, u32[]{:S(2)}, u32[]{:S(2)}) collective-permute-start(bf16[128,1024]{1,0:T(8,128)(2,1)S(1)} %collective-permute-done.34), channel_id=1, source_target_pairs={{4,0},{12,4},{20,12},{28,20},{24,28},{16,24},{8,16},{0,8},{5,1},{1... | collective-permute-start | bytes 786440 | tf_op jit(solution)/shard_map/ppermute | solution.py:64
  448.0 16.9 %collective-permute-start.57 = (bf16[128,1024]{1,0:T(8,128)(2,1)S(1)}, bf16[128,1024]{1,0:T(8,128)(2,1)S(1)}, u32[]{:S(2)}, u32[]{:S(2)}) collective-permute-start(bf16[128,1024]{1,0:T(8,128)(2,1)S(1)} %collective-permute-done.56), channel_id=1, source_target_pairs={{0,4},{4,12},{12,20},{20,28},{28,24},{24,16},{16,8},{8,0},{1,5},{5... | collective-permute-start | bytes 786440 | tf_op jit(solution)/shard_map/ppermute | solution.py:63
  470.5 20.5 %collective-permute-start.65 = (bf16[128,1024]{1,0:T(8,128)(2,1)S(1)}, bf16[128,1024]{1,0:T(8,128)(2,1)S(1)}, u32[]{:S(2)}, u32[]{:S(2)}) collective-permute-start(bf16[128,1024]{1,0:T(8,128)(2,1)S(1)} %collective-permute-done.64), channel_id=1, source_target_pairs={{4,0},{12,4},{20,12},{28,20},{24,28},{16,24},{8,16},{0,8},{5,1},{1... | collective-permute-start | bytes 786440 | tf_op jit(solution)/shard_map/ppermute | solution.py:64
  476.0 20.1 %collective-permute-start.30 = (bf16[128,1024]{1,0:T(8,128)(2,1)S(1)}, bf16[128,1024]{1,0:T(8,128)(2,1)S(1)}, u32[]{:S(2)}, u32[]{:S(2)}) collective-permute-start(bf16[128,1024]{1,0:T(8,128)(2,1)S(1)} %collective-permute-done.29), channel_id=1, source_target_pairs={{0,4},{4,12},{12,20},{20,28},{28,24},{24,16},{16,8},{8,0},{1,5},{5... | collective-permute-start | bytes 786440 | tf_op jit(solution)/shard_map/ppermute | solution.py:63
  476.0 26.0 %collective-permute-start.37 = (bf16[128,1024]{1,0:T(8,128)(2,1)S(1)}, bf16[128,1024]{1,0:T(8,128)(2,1)S(1)}, u32[]{:S(2)}, u32[]{:S(2)}) collective-permute-start(bf16[128,1024]{1,0:T(8,128)(2,1)S(1)} %collective-permute-done.36), channel_id=1, source_target_pairs={{4,0},{12,4},{20,12},{28,20},{24,28},{16,24},{8,16},{0,8},{5,1},{1... | collective-permute-start | bytes 786440 | tf_op jit(solution)/shard_map/ppermute | solution.py:64
  (120 other events, 2071.3 us)
Sparse Core Ops, SparseCore 0:
  62.6 16.5 all-gather.1
  306.2 97.2 all-reduce.3
